TPU v7x, 512 devices: a whole 4x4x16 slice. The times are simulated.
512 devices in a mesh: wall: 32 (over y, x, core), stream: 16 (over z).
Axes of the slice: x: 4, y: 4, z: 16, core: 2. Of those that a mesh axis runs over, the one named last changes fastest.
Arguments:
- cotangent: float32 [5, 16, 1024, 4096], P(None, None, 'wall', 'stream'), may hold values from -6 to 6
- lower: float32 [5, 1024], P(None, 'wall'), may hold values from 0 to 1, as said below
- pivot: float32 [5, 1024], P(None, 'wall'), as said below
- speed: float32 [5, 1024], P(None, 'wall'), may hold values from 0.5 to 2
Outputs:
- state_grad: float32 [5, 16, 1024, 4096], P(None, None, 'wall', 'stream')
Inputs may be any that keep to these rules, and one draw needn't show every extreme that they name: `lower`: every multiplier is strictly between 0 and 1. Every pivot is positive.
All inputs are finite; a program needn't handle non-finite values.
Results may differ from a plain program's by a relative error of at most 0.00012.
Values sent between devices are 32-bit elements; how exact they have to be, the bound alone decides.
No kernel may reach another device: no remote copies, remote signals or barrier semaphores. Data moves between devices by JAX's collectives and lax.ppermute only.
A program may use at most 64 MiB of HBM per device.

v0:
```python
import math

import jax
import jax.numpy as jnp
from jax import lax
from jax.sharding import Mesh
from jax.sharding import PartitionSpec as P

WALL = ("wall_0", "wall_1", "wall_2")


root_value = (math.sqrt(5.0) - 3.0) / 2.0
inverse_gain = 3.0 / math.sqrt(5.0)
first_coeff = 7.0 / 9.0
second_coeff = 1.0 / 36.0


def nothing_yet(array, identity):
    return jax.tree.map(
        lambda a, e: jnp.broadcast_to(jnp.asarray(e, a.dtype), a.shape), array, identity
    )


def carried_in(array, axes, combine, identity, reverse):
    before = start = nothing_yet(array, identity)
    subtotal = array
    for axis in reversed(axes):
        size, place = (lax.axis_size(axis), lax.axis_index(axis))
        pieces = jax.tree.map(lambda part: lax.all_gather(part, axis), subtotal)
        inside, subtotal = (start, start)
        for k in reversed(range(size)) if reverse else range(size):
            passed = k > place if reverse else k < place
            subtotal = combine(subtotal, jax.tree.map(lambda part: part[k], pieces))
            inside = jax.tree.map(lambda new, old: jnp.where(passed, new, old), subtotal, inside)
        before = combine(inside, before)
    return before


def extended_2(cells, sides, width):
    for axis, dim in sides:
        count = lax.axis_size(axis)
        head = lax.slice_in_dim(cells, 0, width, axis=dim)
        tail = lax.slice_in_dim(cells, cells.shape[dim] - width, cells.shape[dim], axis=dim)
        cells = jnp.concatenate(
            [
                lax.ppermute(tail, axis, [(i, (i + 1) % count) for i in range(count)]),
                cells,
                lax.ppermute(head, axis, [((i + 1) % count, i) for i in range(count)]),
            ],
            axis=dim,
        )
    return cells


def compose(earlier, later):
    return (earlier[0] * later[0], later[0] * earlier[1] + later[1])


def decay_power(steps):
    magnitude = jnp.abs(steps)
    parity = jnp.where(magnitude % 2 == 0, 1.0, -1.0).astype(jnp.float32)
    return parity * jnp.exp(magnitude.astype(jnp.float32) * math.log(abs(root_value)))


def build_stencil(length, reach_cells):
    source_index = lax.broadcasted_iota(jnp.int32, (length + 2 * reach_cells, length), 0)
    target_index = lax.broadcasted_iota(jnp.int32, (length + 2 * reach_cells, length), 1)
    offset = source_index - reach_cells - target_index
    values = first_coeff * (decay_power(offset - 1) - decay_power(offset + 1))
    values = values + second_coeff * (decay_power(offset - 2) - decay_power(offset + 2))
    return jnp.where(jnp.abs(offset) <= reach_cells, inverse_gain * values, 0.0)


def apply_stencil(extended, stencil, length):
    flat = extended.reshape((-1, extended.shape[-1]))
    product = jnp.dot(
        flat, stencil, precision=lax.Precision.HIGHEST, preferred_element_type=jnp.float32
    )
    return product.reshape(extended.shape[:-1] + (length,))


def local(cotangent, lower, pivot, speed):
    fields, planes, height, length = cotangent.shape
    log_keep = jnp.log(lower)
    inclusive = jnp.cumsum(log_keep, axis=1)
    exclusive = inclusive - log_keep
    summed = inclusive[:, -1]
    row_index = lax.broadcasted_iota(jnp.int32, (height, height), 0)
    col_index = lax.broadcasted_iota(jnp.int32, (height, height), 1)
    lower_part = (row_index >= col_index)[None]
    exponent = exclusive[:, :, None] - exclusive[:, None, :]
    factor = jnp.where(lower_part, jnp.exp(jnp.where(lower_part, exponent, 0.0)), 0.0)
    rising_base = jnp.einsum("fji,fzix->fzjx", factor, cotangent, precision=lax.Precision.HIGHEST)
    entry_gain = jnp.exp(exclusive)
    leave_gain = jnp.exp(summed[:, None] - exclusive)
    scaled_base = rising_base / pivot[:, None, :, None]
    settle_base = jnp.einsum("fij,fzix->fzjx", factor, scaled_base, precision=lax.Precision.HIGHEST)
    spread = jnp.einsum("fij,fi->fj", factor, entry_gain / pivot, precision=lax.Precision.HIGHEST)
    through = jnp.exp(summed)
    lift_out = lower[:, -1][:, None, None] * rising_base[:, :, -1, :]
    spread_first = spread[:, 0]
    settle_first = settle_base[:, :, 0, :]
    through_map = through[:, None, None]
    identity_pair = (jnp.ones_like(through_map), jnp.zeros_like(lift_out))
    rise_result = carried_in((through_map, lift_out), WALL, compose, identity_pair, False)
    incoming = rise_result[1]
    crest_top = settle_first + incoming * spread_first[:, None, None]
    fall_result = carried_in((through_map, crest_top), WALL, compose, identity_pair, True)
    descent = fall_result[1]
    adjoint = settle_base + incoming[:, :, None, :] * spread[:, None, :, None]
    adjoint = adjoint + descent[:, :, None, :] * leave_gain[:, None, :, None]
    reach_cells = 24
    stencil = build_stencil(length, reach_cells)
    speed_grid = speed[:, None, :, None]
    flux_field = speed_grid * adjoint
    extended = extended_2(flux_field, (("stream", 3),), reach_cells)
    state_grad = adjoint + apply_stencil(extended, stencil, length)
    return state_grad


def solution(mesh):
    finer = Mesh(
        mesh.devices.reshape(4, 4, 2, mesh.shape["stream"]),
        ("wall_0", "wall_1", "wall_2", "stream"),
    )
    return jax.shard_map(
        local,
        mesh=finer,
        in_specs=(P(None, None, WALL, "stream"), P(None, WALL), P(None, WALL), P(None, WALL)),
        out_specs=P(None, None, WALL, "stream"),
        check_vma=False,
    )
```

profile of v0, /device:TPU:8, one launch (start us, length us, event | category | flops | bytes accessed | tf_op | source)
XLA Modules:
  0.0 149.4 jit_solution(3088551716865310269)
XLA Ops:
  3.3 1.3 dynamic-slice
  5.5 2.4 %all-reduce = f32[10]{0:T(128)S(1)} all-reduce(f32[10]{0:T(128)S(1)} %dynamic-update-slice), channel_id=2, replica_groups=mesh['wall_0'=4,'wall_1'=4,'wall_2'=2,'stream'=16] {'wall_2'}, use_global_device_ids=true, to_apply=%add | all-reduce | flops 10 | bytes 80
  7.9 1.3 dynamic-slice.1
  10.0 10.5 %all-reduce.1 = f32[20]{0:T(128)S(1)} all-reduce(f32[20]{0:T(128)S(1)} %multiply_dynamic-update-slice_fusion), channel_id=3, replica_groups=mesh['wall_0'=4,'wall_1'=4,'wall_2'=2,'stream'=16] {'wall_1'}, use_global_device_ids=true, to_apply=%add.1 | all-reduce | flops 20 | bytes 160
  20.5 2.5 %convolution_bitcast_fusion = f32[5,16,32,256]{3,2,1,0:T(8,128)S(1)} fusion(f32[5,16,32,256]{3,2,1,0:T(8,128)S(1)} %copy-done, f32[5,32]{1,0:T(8,128)S(1)} %get-tuple-element.10, pred[32,32]{0,1:T(8,128)(4,1)S(1)} %iota_compare_fusion), kind=kOutput, calls=%fused_computation.12 | convolution fusion | flops 251673600 | bytes 5244544 | tf_op jit(solution)/shard_map/fji,fzix->fzjx/dot_general | solution.py:93
  23.0 2.6 %fusion.12 = f32[5,16,32,256]{3,2,1,0:T(8,128)S(1)} fusion(f32[5,16,32,256]{3,2,1,0:T(8,128)S(1)} %convolution_bitcast_fusion, f32[5,32]{1,0:T(8,128)S(1)} %copy-done.4, f32[5,32]{1,0:T(8,128)S(1)} %get-tuple-element.10, pred[32,32]{0,1:T(8,128)(4,1)S(1)} %iota_compare_fusion), kind=kOutput, calls=%fused_computation.11 | convolution fusion | flops 252328960 | bytes 5245184 | tf_op jit(solution)/shard_map/fij,fzix->fzjx/dot_general | solution.py:97
  25.8 1.9 %all_gather.45 = f32[2,5,16,256]{3,2,1,0:T(8,128)S(1)} all-gather(f32[1,5,16,256]{3,2,1,0:T(8,128)S(1)} %copy.24), channel_id=1, replica_groups=mesh['wall_0'=4,'wall_1'=4,'wall_2'=2,'stream'=16] {'wall_2'}, dimensions={0}, use_global_device_ids=true | all-gather | bytes 245760 | tf_op jit(solution)/shard_map/all_gather | solution.py:29
  27.9 12.7 %all_gather.46 = f32[4,5,16,256]{3,2,1,0:T(8,128)S(1)} all-gather(f32[1,5,16,256]{3,2,1,0:T(8,128)S(1)} %get-tuple-element.17), channel_id=1, replica_groups=mesh['wall_0'=4,'wall_1'=4,'wall_2'=2,'stream'=16] {'wall_1'}, dimensions={0}, use_global_device_ids=true | all-gather | bytes 409600 | tf_op jit(solution)/shard_map/all_gather | solution.py:29
  40.9 12.8 %all_gather.47 = f32[4,5,16,256]{3,2,1,0:T(8,128)S(1)} all-gather(f32[1,5,16,256]{3,2,1,0:T(8,128)S(1)} %copy.27), channel_id=1, replica_groups=mesh['wall_0'=4,'wall_1'=4,'wall_2'=2,'stream'=16] {'wall_0'}, dimensions={0}, use_global_device_ids=true | all-gather | bytes 409600 | tf_op jit(solution)/shard_map/all_gather | solution.py:29
  53.7 9.3 %all_gather.44 = f32[4,5,1,1]{1,3,2,0:T(1,128)S(1)} all-gather(f32[1,5,1,1]{1,3,2,0:T(1,128)S(1)} %get-tuple-element.31), channel_id=1, replica_groups=mesh['wall_0'=4,'wall_1'=4,'wall_2'=2,'stream'=16] {'wall_0'}, dimensions={0}, use_global_device_ids=true | all-gather | bytes 100 | tf_op jit(solution)/shard_map/all_gather | solution.py:29
  63.9 1.9 %all_gather.49 = f32[2,5,16,256]{3,2,1,0:T(8,128)S(1)} all-gather(f32[1,5,16,256]{3,2,1,0:T(8,128)S(1)} %copy.36), channel_id=1, replica_groups=mesh['wall_0'=4,'wall_1'=4,'wall_2'=2,'stream'=16] {'wall_2'}, dimensions={0}, use_global_device_ids=true | all-gather | bytes 245760 | tf_op jit(solution)/shard_map/all_gather | solution.py:29
  65.9 12.4 %all_gather.50 = f32[4,5,16,256]{3,2,1,0:T(8,128)S(1)} all-gather(f32[1,5,16,256]{3,2,1,0:T(8,128)S(1)} %multiply_add_fusion.2), channel_id=1, replica_groups=mesh['wall_0'=4,'wall_1'=4,'wall_2'=2,'stream'=16] {'wall_1'}, dimensions={0}, use_global_device_ids=true | all-gather | bytes 409600 | tf_op jit(solution)/shard_map/all_gather | solution.py:29
  78.4 11.2 %all_gather.51 = f32[4,5,16,256]{3,2,1,0:T(8,128)S(1)} all-gather(f32[1,5,16,256]{3,2,1,0:T(8,128)S(1)} %multiply_add_fusion.1), channel_id=1, replica_groups=mesh['wall_0'=4,'wall_1'=4,'wall_2'=2,'stream'=16] {'wall_0'}, dimensions={0}, use_global_device_ids=true | all-gather | bytes 409600 | tf_op jit(solution)/shard_map/all_gather | solution.py:29
  89.6 9.0 %all_gather.48 = f32[4,5,1,1]{1,3,2,0:T(1,128)S(1)} all-gather(f32[1,5,1,1]{1,3,2,0:T(1,128)S(1)} %get-tuple-element.30), channel_id=1, replica_groups=mesh['wall_0'=4,'wall_1'=4,'wall_2'=2,'stream'=16] {'wall_0'}, dimensions={0}, use_global_device_ids=true | all-gather | bytes 100 | tf_op jit(solution)/shard_map/all_gather | solution.py:29
  99.7 2.3 %fusion.144 = (f32[5,16,32,24]{3,2,1,0:T(8,128)}, f32[5,16,32,24]{3,2,1,0:T(8,128)}) fusion(f32[5,16,32,256]{3,2,1,0:T(8,128)S(1)} %fusion.9), kind=kLoop, calls=%fused_computation.234 | loop fusion | bytes 983040 | tf_op jit(solution)/shard_map/slice | solution.py:43
  102.0 2.7 %copy.37 = f32[5,16,32,24]{2,3,1,0:T(8,128)} copy(f32[5,16,32,24]{3,2,1,0:T(8,128)} %get-tuple-element.19) | data formatting | bytes 491520 | tf_op jit(solution)/shard_map/slice | solution.py:43
  104.7 3.9 %collective-permute-start = (f32[5,16,32,24]{2,3,1,0:T(8,128)}, f32[5,16,32,24]{2,3,1,0:T(8,128)}, u32[]{:S(2)}, u32[]{:S(2)}) collective-permute-start(f32[5,16,32,24]{2,3,1,0:T(8,128)} %copy.37), channel_id=1, source_target_pairs={{0,1},{1,2},{2,3},{3,4},{4,5},{5,6},{6,7},{7,8},{8,9},{9,10},{10,1... | collective-permute-start | bytes 737288 | tf_op jit(solution)/shard_map/ppermute | solution.py:46
  108.6 2.7 %copy.38 = f32[5,16,32,24]{2,3,1,0:T(8,128)} copy(f32[5,16,32,24]{3,2,1,0:T(8,128)} %get-tuple-element.20) | data formatting | bytes 491520 | tf_op jit(solution)/shard_map/slice | solution.py:42
  111.3 9.7 %collective-permute-start.1 = (f32[5,16,32,24]{2,3,1,0:T(8,128)}, f32[5,16,32,24]{2,3,1,0:T(8,128)}, u32[]{:S(2)}, u32[]{:S(2)}) collective-permute-start(f32[5,16,32,24]{2,3,1,0:T(8,128)} %copy.38), channel_id=1, source_target_pairs={{1,0},{2,1},{3,2},{4,3},{5,4},{6,5},{7,6},{8,7},{9,8},{10,9},{11,1... | collective-permute-start | bytes 737288 | tf_op jit(solution)/shard_map/ppermute | solution.py:48
  121.0 10.9 %collective-permute-done = f32[5,16,32,24]{2,3,1,0:T(8,128)} collective-permute-done((f32[5,16,32,24]{2,3,1,0:T(8,128)}, f32[5,16,32,24]{2,3,1,0:T(8,128)}, u32[]{:S(2)}, u32[]{:S(2)}) %collective-permute-start) | collective-permute-done | bytes 245792 | tf_op jit(solution)/shard_map/ppermute | solution.py:46
  131.8 2.7 %copy.39 = f32[5,16,32,24]{3,2,1,0:T(8,128)} copy(f32[5,16,32,24]{2,3,1,0:T(8,128)} %collective-permute-done) | data formatting | bytes 491520 | tf_op jit(solution)/shard_map/ppermute | solution.py:46
  134.6 1.1 collective-permute-done.1
  135.7 2.7 %copy.40 = f32[5,16,32,24]{3,2,1,0:T(8,128)} copy(f32[5,16,32,24]{2,3,1,0:T(8,128)} %collective-permute-done.1) | data formatting | bytes 491520 | tf_op jit(solution)/shard_map/ppermute | solution.py:48
  138.4 11.0 %fusion.8 = f32[5,16,32,256]{3,2,1,0:T(8,128)} fusion(f32[5,16,32,256]{3,2,1,0:T(8,128)} %copy-done.2, f32[5,16,32,24]{3,2,1,0:T(8,128)} %copy.40, f32[5,16,32,256]{3,2,1,0:T(8,128)} %copy-done.1, f32[5,16,32,24]{3,2,1,0:T(8,128)} %copy.39, f32[5,32]{1,0:T(8,128)S(1)} %subtract_exponential_fusion, f32[5,16,256]{2,1,0:T(8,128)S(1)} %fusion.88, ...), kind=kOutput, calls=%fused_computation.9 | convolution fusion | flops 2401968128 | bytes 8522176 | tf_op jit(solution)/shard_map/dot_general | solution.py:76
  (45 shorter events, 6.4 us)
Async XLA Ops:
  0.0 20.5 %copy-start = (f32[5,16,32,256]{3,2,1,0:T(8,128)S(1)}, f32[5,16,32,256]{3,2,1,0:T(8,128)}, u32[]{:S(2)}) copy-start(f32[5,16,32,256]{3,2,1,0:T(8,128)} %param.4) | copy-start | bytes 7864324
  20.5 2.5 %copy-start.4 = (f32[5,32]{1,0:T(8,128)S(1)}, f32[5,32]{1,0:T(8,128)}, u32[]{:S(2)}) copy-start(f32[5,32]{1,0:T(8,128)} %param.6) | copy-start | bytes 1924
  25.6 73.2 %copy-start.2 = (f32[5,16,32,256]{3,2,1,0:T(8,128)}, f32[5,16,32,256]{3,2,1,0:T(8,128)S(1)}, u32[]{:S(2)}) copy-start(f32[5,16,32,256]{3,2,1,0:T(8,128)S(1)} %fusion.12) | copy-start | bytes 7864324
  40.9 57.9 %copy-start.3 = (f32[5,32]{1,0:T(8,128)S(1)}, f32[5,32]{1,0:T(8,128)}, u32[]{:S(2)}) copy-start(f32[5,32]{1,0:T(8,128)} %param.7) | copy-start | bytes 1924
  99.7 2.3 %copy-start.1 = (f32[5,16,32,256]{3,2,1,0:T(8,128)}, f32[5,16,32,256]{3,2,1,0:T(8,128)S(1)}, u32[]{:S(2)}) copy-start(f32[5,16,32,256]{3,2,1,0:T(8,128)S(1)} %fusion.9) | copy-start | bytes 7864324
  104.7 27.1 %collective-permute-start = (f32[5,16,32,24]{2,3,1,0:T(8,128)}, f32[5,16,32,24]{2,3,1,0:T(8,128)}, u32[]{:S(2)}, u32[]{:S(2)}) collective-permute-start(f32[5,16,32,24]{2,3,1,0:T(8,128)} %copy.37), channel_id=1, source_target_pairs={{0,1},{1,2},{2,3},{3,4},{4,5},{5,6},{6,7},{7,8},{8,9},{9,10},{10,1... | collective-permute-start | bytes 737288 | tf_op jit(solution)/shard_map/ppermute | solution.py:46
  111.3 24.4 %collective-permute-start.1 = (f32[5,16,32,24]{2,3,1,0:T(8,128)}, f32[5,16,32,24]{2,3,1,0:T(8,128)}, u32[]{:S(2)}, u32[]{:S(2)}) collective-permute-start(f32[5,16,32,24]{2,3,1,0:T(8,128)} %copy.38), channel_id=1, source_target_pairs={{1,0},{2,1},{3,2},{4,3},{5,4},{6,5},{7,6},{8,7},{9,8},{10,9},{11,1... | collective-permute-start | bytes 737288 | tf_op jit(solution)/shard_map/ppermute | solution.py:48
where the time goes:
time: 150 us; the launch traced here: 149 us
  blocking collectives  84.1 us (56%)
  local copies, waits for them, and re-layouts  17.9 us (12%)
  matrix products  16.5 us (11%)
  starting transfers between devices  13.6 us (9%)
  waiting for transfers between devices  12 us (8%)
  other arithmetic  3.77 us (3%)
  between operations  1.58 us (1%)
    all_gather x8, blocking collectives, carried_in(): pieces = jax.tree.map(lambda part: lax.all_gather(part, axis), subtotal)  71.2 us
    unnamed x2, blocking collectives  12.9 us
    dot_general x1, matrix products, apply_stencil(): jnp.dot(flat, stencil, precision=lax.Precision.HIGHEST, preferred_element...  11 us
    ppermute x1, waiting for transfers between devices, extended_2(): lax.ppermute(tail, axis, [(i, (i + 1) % count) for i in range(count)])  10.9 us
    ppermute x1, starting transfers between devices, extended_2(): lax.ppermute(head, axis, [((i + 1) % count, i) for i in range(count)])  9.67 us
    slice x2, local copies, waits for them, and re-layouts, extended_2(): lax.slice_in_dim(cells, cells.shape[dim] - width, cells.shape[dim], axis=...  4.95 us
    ppermute x1, starting transfers between devices, extended_2(): lax.ppermute(tail, axis, [(i, (i + 1) % count) for i in range(count)])  3.9 us
  transfers between devices with their start and end apart: 2, of which 2 were waited for; matrix products, arithmetic and copies ran while one was open for 4% of the time, Pallas kernels for 0%

commit v1 on v0

v1 whole, which is shorter than its diff:
```python
import math

import jax
import jax.numpy as jnp
import ml_dtypes
import numpy as np
from jax import lax
from jax.experimental import pallas as pl
from jax.experimental.pallas import tpu as pltpu
from jax.sharding import PartitionSpec as P

F32, BF16 = jnp.float32, jnp.bfloat16
R = (math.sqrt(5.0) - 3.0) / 2.0
GAIN = 3.0 / math.sqrt(5.0)
C1 = 7.0 / 9.0
C2 = 1.0 / 36.0
FIELDS, PLANES, ROWS, CELLS, WALLS = 5, 16, 32, 256, 32


def split_np(w):
    w = np.asarray(w, np.float64)
    hi = w.astype(ml_dtypes.bfloat16)
    lo = (w - hi.astype(np.float64)).astype(ml_dtypes.bfloat16)
    return hi, lo


def tables():
    dec = lambda n: np.where(np.abs(n) % 2 == 0, 1.0, -1.0) * np.abs(R) ** np.abs(n)
    off = np.arange(CELLS)[:, None] - np.arange(CELLS)[None, :]
    tap = lambda o: GAIN * (C1 * (dec(o - 1) - dec(o + 1)) + C2 * (dec(o - 2) - dec(o + 2)))
    whi, wlo = split_np(tap(off))
    kappa = GAIN * (C1 * (1.0 / R - R) + C2 * (R**-2 - R**2))
    corr = tap(np.array(-1)) + kappa * R
    x = np.arange(CELLS)
    ext = np.zeros((4, CELLS))
    ext[0] = kappa * dec(CELLS - x)
    ext[1, CELLS - 1] = -corr
    ext[2] = -kappa * dec(x + 1)
    ext[3, 0] = corr
    ehi, elo = split_np(np.repeat(ext, PLANES, axis=0))
    zero = np.zeros_like(elo)
    stencil = np.concatenate([whi, whi, wlo, ehi, elo, ehi, zero], axis=0)
    edge = np.zeros((CELLS, 4))
    edge[:, 0] = dec(x)
    edge[0, 1] = 1.0
    edge[:, 2] = dec(CELLS - 1 - x)
    edge[CELLS - 1, 3] = 1.0
    edge = np.concatenate([np.repeat(edge, PLANES, axis=1), np.zeros((CELLS, 64))], axis=1)
    ghi, glo = split_np(edge)
    return stencil, np.concatenate([ghi, ghi, glo], axis=0)


def halves(x):
    hi = x.astype(BF16)
    return hi, (x - hi.astype(F32)).astype(BF16)


def lanes(shape):
    return lax.broadcasted_iota(jnp.int32, shape, len(shape) - 1)


def sublanes(shape):
    return lax.broadcasted_iota(jnp.int32, shape, len(shape) - 2)


def edge_kernel(c_ref, w_ref, left_ref, right_ref):
    w = w_ref[...]
    lane32, lane = lanes((ROWS, 128)) % 16, lanes((8, 128)) // 32
    for f in range(FIELDS):
        tiles = c_ref[f].reshape(PLANES * 4, 2, 8, 128)
        rows = [tiles[:, h].reshape(PLANES * ROWS, 128) for h in range(2)]
        hi, lo = halves(jnp.concatenate(rows, axis=1))
        sums = jnp.dot(jnp.concatenate([hi, lo, hi], axis=1), w, preferred_element_type=F32)
        own = sums[:ROWS]
        for p in range(1, PLANES):
            own = jnp.where(lane32 == p, sums[p * ROWS : (p + 1) * ROWS], own)
        left = own[:8]
        right = pltpu.roll(own[:8], 96, 1)
        for q in range(1, 4):
            part = own[8 * q : 8 * q + 8]
            left = jnp.where(lane == q, pltpu.roll(part, 32 * q, 1), left)
            right = jnp.where(lane == q, pltpu.roll(part, (32 * q + 96) % 128, 1) if q != 1 else part, right)
        left_ref[f] = left
        right_ref[f] = right


def row_of(j, h):
    return (j // 8) * 16 + h * 8 + j % 8


def load_row(ref, f, j):
    return jnp.concatenate([ref[f, pl.ds(row_of(j, h), PLANES, stride=64), :] for h in range(2)], 1)


def spread_rows(ref, out_ref):
    value = ref[...]
    for j in range(ROWS):
        out_ref[j * 8 : j * 8 + FIELDS, :] = jnp.broadcast_to(value[:, j : j + 1], (FIELDS, 128))


def sums_kernel(c_ref, lower_ref, pivot_ref, out_ref, rise_ref, fall_ref, unit_ref):
    low, piv = lower_ref[...], pivot_ref[...]
    wide = lambda v, j: jnp.broadcast_to(v[:, j : j + 1], (FIELDS, 128))
    entry = jnp.ones((FIELDS, 128), F32)
    entries, inverse, spread = [], [], jnp.zeros((FIELDS, 128), F32)
    for j in range(ROWS):
        inverse.append(1.0 / wide(piv, j))
        entries.append(entry)
        spread = spread + entry * entry * inverse[j]
        entry = entry * wide(low, j)
    leave, first = None, None
    for j in reversed(range(ROWS)):
        l = wide(low, j)
        leave = l if leave is None else l * leave
        first = entries[j] * inverse[j] if first is None else entries[j] * inverse[j] + l * first
        rise_ref[j * 8 : j * 8 + FIELDS, :] = leave
        fall_ref[j * 8 : j * 8 + FIELDS, :] = first
    unit_ref[0, :FIELDS, :] = entry
    unit_ref[1, :FIELDS, :] = spread
    for f in range(FIELDS):
        up = jnp.zeros((PLANES, CELLS), F32)
        down = jnp.zeros((PLANES, CELLS), F32)
        for j in range(ROWS):
            v = load_row(c_ref, f, j)
            a = rise_ref[pl.ds(j * 8 + f, 8, stride=0), :]
            b = fall_ref[pl.ds(j * 8 + f, 8, stride=0), :]
            a = jnp.concatenate([jnp.concatenate([a, a], 0)] * 2, 1)
            b = jnp.concatenate([jnp.concatenate([b, b], 0)] * 2, 1)
            up = up + a * v
            down = down + b * v
        for h in range(2):
            for q in range(2):
                base = (16 * q + h) * 16 + f
                out_ref[pl.ds(base, 8, stride=32), :] = up[8 * q : 8 * q + 8, 128 * h : 128 * h + 128]
                out_ref[pl.ds(base + 8, 8, stride=32), :] = down[8 * q : 8 * q + 8, 128 * h : 128 * h + 128]


def merge_kernel(main_ref, rise_ref, fall_ref, unit_ref, left_ref, right_ref, out_ref, ext_ref):
    lane = lanes((8, 128))
    ups, downs = [], []
    for f in range(FIELDS):
        up = jnp.zeros((8, 128), F32)
        down = jnp.zeros((8, 128), F32)
        from_left, from_right = left_ref[f], right_ref[f]
        for q in range(4):
            r = pltpu.roll(from_right, (128 - 32 * q) % 128, 1) if q else from_right
            l = pltpu.roll(from_left, (128 - 32 * q + 32) % 128, 1) if q != 1 else from_left
            v = jnp.where(lane < 32, r, l)
            v = jnp.where(lane < 64, v, pltpu.roll(v, 64, 1))
            ext_ref[f, 8 * q : 8 * q + 8, :] = v
            up = up + rise_ref[pl.ds(64 * q + f, 8, stride=8), :] * v
            down = down + fall_ref[pl.ds(64 * q + f, 8, stride=8), :] * v
        ups.append(jnp.sum(up, axis=0, keepdims=True))
        downs.append(jnp.sum(down, axis=0, keepdims=True))
    for f in range(FIELDS, 8):
        ext_ref[f] = jnp.zeros((ROWS, 128), F32)
    row = sublanes((FIELDS, 128))
    lane5 = lanes((FIELDS, 128))
    coef = jnp.where(lane5 == 64 + row, unit_ref[0, :FIELDS, :], 0.0)
    coef = jnp.where(lane5 == 72 + row, unit_ref[1, :FIELDS, :], coef)
    coef = jnp.sum(coef, axis=0, keepdims=True)
    lane1 = lanes((1, 128))
    sub = sublanes((8, 128))

    def pack(v, last):
        rows = [jnp.where(lane1 < 64, v[0], v[1]), jnp.where(lane1 < 64, v[2], v[3]), jnp.where(lane1 < 64, v[4], last)]
        return jnp.where(sub == 5, rows[0], jnp.where(sub == 6, rows[1], rows[2]))

    tail_up, tail_down = pack(ups, coef), pack(downs, jnp.zeros((1, 128), F32))
    for k in range(WALLS):
        out_ref[k, :8, :] = jnp.where(sub < 5, main_ref[16 * k : 16 * k + 8, :], tail_up)
        out_ref[k, 8:, :] = jnp.where(sub < 5, main_ref[16 * k + 8 : 16 * k + 16, :], tail_down)


def carry_kernel(in_ref, out_ref, through_ref, crest_ref):
    sub, lane = sublanes((8, 128)), lanes((8, 128))
    low_field = jnp.where(sub < 5, sub, 2 * (sub - 5))
    high_field = jnp.where(sub < 5, sub, jnp.where(sub < 7, 2 * (sub - 5) + 1, 4))

    def pick(row, at):
        lo = jnp.sum(jnp.where(lane == at + low_field, row, 0.0), axis=1, keepdims=True)
        hi = jnp.sum(jnp.where(lane == at + high_field, row, 0.0), axis=1, keepdims=True)
        return jnp.where(lane < 64, lo, hi)

    run = jnp.zeros((8, 128), F32)
    for d in range(WALLS):
        row = jnp.broadcast_to(in_ref[d, 7:8, :], (8, 128))
        through, spread = pick(row, 64), pick(row, 72)
        through_ref[d] = through
        out_ref[d, :8, :] = run
        crest_ref[d] = in_ref[d, 8:, :] + spread * run
        run = through * run + in_ref[d, :8, :]
    run = jnp.zeros((8, 128), F32)
    for d in reversed(range(WALLS)):
        out_ref[d, 8:, :] = run
        run = through_ref[d] * run + crest_ref[d]


def final_kernel(c_ref, ret_ref, lower_ref, pivot_ref, speed_ref, ext_ref, w_ref, o_ref, low_ref, inv_ref, sp_ref, fe_ref, sc_ref, lhs_ref, res_ref, sem):
    spread_rows(lower_ref, low_ref)
    spread_rows(speed_ref, sp_ref)
    value = 1.0 / pivot_ref[...]
    for j in range(ROWS):
        inv_ref[j * 8 : j * 8 + FIELDS, :] = jnp.broadcast_to(value[:, j : j + 1], (FIELDS, 128))
    sub, lane = sublanes((8, 128)), lanes((8, 128))

    def unpack(tile):
        turned = pltpu.roll(tile, 64, 1)
        a, b = jnp.where(lane < 64, tile, turned), jnp.where(lane < 64, turned, tile)
        rows = [a[5:6], b[5:6], a[6:7], b[6:7], a[7:8]]
        out = jnp.broadcast_to(rows[4], (8, 128))
        for f in range(4):
            out = jnp.where(sub == f, rows[f], out)
        return jnp.where(sub < FIELDS, out, 0.0)

    run = unpack(ret_ref[0:8, :])
    for j in range(ROWS):
        run = ext_ref[pl.ds(j, 8, stride=ROWS), :] + run
        fe_ref[j * 8 : j * 8 + 8, :] = run * inv_ref[j * 8 : j * 8 + 8, :]
        run = run * low_ref[j * 8 : j * 8 + 8, :]
    run = unpack(ret_ref[8:16, :])
    for j in reversed(range(ROWS)):
        run = fe_ref[j * 8 : j * 8 + 8, :] + low_ref[j * 8 : j * 8 + 8, :] * run
        fe_ref[j * 8 : j * 8 + 8, :] = run * sp_ref[j * 8 : j * 8 + 8, :]

    mine = lanes((PLANES, 128)) % 16 == sublanes((PLANES, 128))
    w = w_ref[...]

    def full(ref, j, f):
        v = ref[pl.ds(j * 8 + f, 8, stride=0), :]
        return jnp.concatenate([jnp.concatenate([v, v], 0)] * 2, 1)

    copies = []
    for f in range(FIELDS):
        slot = f % 2

        def carry(shift):
            parts = [
                [ret_ref[pl.ds((16 * q + h) * 16 + f + shift, 8, stride=32), :] for h in range(2)] for q in range(2)
            ]
            return jnp.concatenate([jnp.concatenate(p, 1) for p in parts], 0)

        run = carry(0)
        for j in range(ROWS):
            run = load_row(c_ref, f, j) + run
            sc_ref[slot, j * 16 : j * 16 + 16, :] = run * full(inv_ref, j, f)
            run = run * full(low_ref, j, f)
        run = carry(8)
        for j in reversed(range(ROWS)):
            run = sc_ref[slot, j * 16 : j * 16 + 16, :] + full(low_ref, j, f) * run
            sc_ref[slot, j * 16 : j * 16 + 16, :] = run
            hi, lo = halves(run * full(sp_ref, j, f))
            e = fe_ref[pl.ds(j * 8 + f, 8, stride=0), :]
            ehi, elo = halves(jnp.where(mine, jnp.concatenate([e, e], 0), 0.0))
            lhs_ref[slot, j * 16 : j * 16 + 16, :] = jnp.concatenate([hi, lo, hi, ehi, elo], 1)
        out = sc_ref[slot] + jnp.dot(lhs_ref[slot], w, preferred_element_type=F32)
        for j in range(ROWS):
            for h in range(2):
                res_ref[f, pl.ds(row_of(j, h), PLANES, stride=64), :] = out[j * 16 : j * 16 + 16, 128 * h : 128 * h + 128]
        copy = pltpu.make_async_copy(res_ref.at[f], o_ref.at[f], sem.at[f])
        copy.start()
        copies.append(copy)
    for copy in copies:
        copy.wait()


def params():
    return pltpu.CompilerParams(vmem_limit_bytes=24 * 1024 * 1024)


VM = pl.BlockSpec(memory_space=pltpu.VMEM)


def local(cotangent, lower, pivot, speed):
    stencil, edge = tables()
    sds = jax.ShapeDtypeStruct
    flat = cotangent.reshape(FIELDS, PLANES, 4, 8, 2, 128).transpose(0, 1, 2, 4, 3, 5).reshape(FIELDS, 1024, 128)
    left, right = pl.pallas_call(
        edge_kernel,
        out_shape=[sds((FIELDS, 8, 128), F32)] * 2,
        in_specs=[VM] * 2,
        out_specs=[VM] * 2,
        compiler_params=params(),
        name="edge",
    )(flat, jnp.asarray(edge))
    count = lax.axis_size("stream")
    from_left = lax.ppermute(right, "stream", [(i, (i + 1) % count) for i in range(count)])
    from_right = lax.ppermute(left, "stream", [((i + 1) % count, i) for i in range(count)])
    main, rise, fall, unit = pl.pallas_call(
        sums_kernel,
        out_shape=[sds((WALLS * 16, 128), F32), sds((ROWS * 8, 128), F32), sds((ROWS * 8, 128), F32), sds((2, 8, 128), F32)],
        in_specs=[VM] * 3,
        out_specs=[VM] * 4,
        compiler_params=params(),
        cost_estimate=pl.CostEstimate(flops=4000000, bytes_accessed=2600000, transcendentals=0),
        name="sums",
    )(flat, lower, pivot)
    send, ext = pl.pallas_call(
        merge_kernel,
        out_shape=[sds((WALLS, 16, 128), F32), sds((8, ROWS, 128), F32)],
        in_specs=[VM] * 6,
        out_specs=[VM] * 2,
        compiler_params=params(),
        name="merge",
    )(main, rise, fall, unit, from_left, from_right)
    got = lax.all_to_all(send, "wall", 0, 0, tiled=True)
    carries = pl.pallas_call(
        carry_kernel,
        out_shape=sds((WALLS, 16, 128), F32),
        in_specs=[VM],
        out_specs=VM,
        scratch_shapes=[pltpu.VMEM((WALLS, 8, 128), F32)] * 2,
        compiler_params=params(),
        name="carry",
    )(got)
    back = lax.all_to_all(carries, "wall", 0, 0, tiled=True)
    out = pl.pallas_call(
        final_kernel,
        out_shape=sds((FIELDS, 1024, 128), F32),
        in_specs=[VM] * 7,
        out_specs=pl.BlockSpec(memory_space=pl.ANY),
        scratch_shapes=[pltpu.VMEM((ROWS * 8, 128), F32)] * 4
        + [
            pltpu.VMEM((2, ROWS * PLANES, CELLS), F32),
            pltpu.VMEM((2, ROWS * PLANES, 1024), BF16),
            pltpu.VMEM((FIELDS, 1024, 128), F32),
            pltpu.SemaphoreType.DMA((FIELDS,)),
        ],
        compiler_params=params(),
        name="final",
    )(flat, back.reshape(WALLS * 16, 128), lower, pivot, speed, ext.reshape(8 * ROWS, 128), jnp.asarray(stencil))
    return out.reshape(FIELDS, PLANES, 4, 2, 8, 128).transpose(0, 1, 2, 4, 3, 5).reshape(FIELDS, PLANES, ROWS, CELLS)


def solution(mesh):
    return jax.shard_map(
        local,
        mesh=mesh,
        in_specs=(P(None, None, "wall", "stream"), P(None, "wall"), P(None, "wall"), P(None, "wall")),
        out_specs=P(None, None, "wall", "stream"),
        check_vma=False,
    )
```

time: 150 us -> 55.9 us (0.37)
  the two profiles are of different devices: /device:TPU:8 before, /device:TPU:1 now
where the time goes in v1:
time: 55.9 us; the launch traced here: 55.7 us
  blocking collectives  29.1 us (52%)
  starting transfers between devices  14.1 us (25%)
  Pallas kernels  9.62 us (17%)
  local copies, waits for them, and re-layouts  2.69 us (5%)
    all_to_all x1, blocking collectives, local(): got = lax.all_to_all(send, 'wall', 0, 0, tiled=True)  16.7 us
    all_to_all x1, blocking collectives, local(): back = lax.all_to_all(carries, 'wall', 0, 0, tiled=True)  12.4 us
    ppermute x1, starting transfers between devices, local(): lax.ppermute(left, 'stream', [((i + 1) % count, i) for i in range(count)])  9.5 us
    pallas_call x1, Pallas kernels, local(): pl.pallas_call(final_kernel, out_shape=sds((FIELDS, 1024, 128), F32), in_...  6.21 us
    ppermute x1, starting transfers between devices, local(): lax.ppermute(right, 'stream', [(i, (i + 1) % count) for i in range(count)])  4.63 us
    unnamed x14, local copies, waits for them, and re-layouts  2.69 us
    pallas_call x1, Pallas kernels, local(): pl.pallas_call(sums_kernel, out_shape=[sds((WALLS * 16, 128), F32), sds((...  1.74 us
    pallas_call x1, Pallas kernels, local(): pl.pallas_call(edge_kernel, out_shape=[sds((FIELDS, 8, 128), F32)] * 2, i...  1.26 us
  transfers between devices with their start and end apart: 2, of which 0 were waited for; matrix products, arithmetic and copies ran while one was open for 0% of the time, Pallas kernels for 3%

profile of v1, /device:TPU:1, one launch (start us, length us, event | category | flops | bytes accessed | tf_op | source)
XLA Modules:
  0.0 55.7 jit_solution(17237965589942984360)
XLA Ops:
  0.0 0.0 copy-start
  0.0 1.7 %copy-done = f32[5,16,32,256]{3,2,1,0:T(8,128)S(1)} copy-done((f32[5,16,32,256]{3,2,1,0:T(8,128)S(1)}, f32[5,16,32,256]{3,2,1,0:T(8,128)}, u32[]{:S(2)}) %copy-start) | copy-done | bytes 2621464
  1.7 0.0 copy-start.3
  1.7 0.9 %copy-done.3 = bf16[768,128]{1,0:T(8,128)(2,1)S(1)} copy-done((bf16[768,128]{1,0:T(8,128)(2,1)S(1)}, bf16[768,128]{1,0:T(8,128)(2,1)}, u32[]{:S(2)}) %copy-start.3) | copy-done | bytes 196632
  2.7 0.0 copy-start.4
  2.7 1.3 %edge.1 = (f32[5,8,128]{2,1,0:T(8,128)S(1)}, f32[5,8,128]{2,1,0:T(8,128)S(1)}) custom-call(f32[5,1024,128]{2,1,0:T(8,128)S(1)} %bitcast.12, bf16[768,128]{1,0:T(8,128)(2,1)S(1)} %copy-done.3), custom_call_target="tpu_custom_call" | custom-call | tf_op jit(solution)/shard_map/edge/pallas_call | solution.py:278
  3.9 0.0 copy-start.1
  3.9 0.0 copy-start.2
  4.0 0.0 copy-start.6
  4.0 4.6 %collective-permute-start = (f32[5,8,128]{2,1,0:T(8,128)S(1)}, f32[5,8,128]{2,1,0:T(8,128)S(1)}, u32[]{:S(2)}, u32[]{:S(2)}) collective-permute-start(f32[5,8,128]{2,1,0:T(8,128)S(1)} %get-tuple-element.17), channel_id=1, source_target_pairs={{0,1},{1,2},{2,3},{3,4},{4,5},{5,6},{6,7},{7,8},{8,9},{9,10},{10,1... | collective-permute-start | bytes 61448 | tf_op jit(solution)/shard_map/ppermute | solution.py:287
  8.6 9.5 %collective-permute-start.1 = (f32[5,8,128]{2,1,0:T(8,128)S(1)}, f32[5,8,128]{2,1,0:T(8,128)S(1)}, u32[]{:S(2)}, u32[]{:S(2)}) collective-permute-start(f32[5,8,128]{2,1,0:T(8,128)S(1)} %get-tuple-element.18), channel_id=1, source_target_pairs={{1,0},{2,1},{3,2},{4,3},{5,4},{6,5},{7,6},{8,7},{9,8},{10,9},{11,1... | collective-permute-start | bytes 61448 | tf_op jit(solution)/shard_map/ppermute | solution.py:288
  18.1 0.0 copy-done.4
  18.1 0.0 copy-done.5
  18.1 1.7 %sums.1 = (f32[512,128]{1,0:T(8,128)S(1)}, f32[256,128]{1,0:T(8,128)S(1)}, f32[256,128]{1,0:T(8,128)S(1)}, f32[2,8,128]{2,1,0:T(8,128)S(1)}) custom-call(f32[5,1024,128]{2,1,0:T(8,128)S(1)} %bitcast.13, f32[5,32]{1,0:T(8,128)S(1)} %copy-done.4, f32[5,32]{1,0:T(8,128)S(1)} %copy-done.5), custom_call_target="tpu_custom_call" | custom-call | flops 4000000 | bytes 2600000 | tf_op jit(solution)/shard_map/sums/pallas_call | solution.py:289
  19.9 0.0 collective-permute-done.left_ref
  19.9 0.0 collective-permute-done.1.right_ref
  19.9 0.2 merge.1
  20.1 16.7 %all_to_all.10.in_ref = f32[32,16,128]{2,1,0:T(8,128)S(1)} all-to-all(f32[32,16,128]{2,1,0:T(8,128)S(1)} %get-tuple-element.19), channel_id=1, replica_groups=mesh['wall'=32,'stream'=16] {'wall'}, dimensions={0} | all-to-all | bytes 524288 | tf_op jit(solution)/shard_map/all_to_all | solution.py:306
  36.8 0.2 carry.1
  37.0 12.4 %all_to_all.11 = f32[32,16,128]{2,1,0:T(8,128)S(1)} all-to-all(f32[32,16,128]{2,1,0:T(8,128)S(1)} %carry.1), channel_id=1, replica_groups=mesh['wall'=32,'stream'=16] {'wall'}, dimensions={0} | all-to-all | bytes 524288 | tf_op jit(solution)/shard_map/all_to_all | solution.py:316
  49.5 0.0 copy-done.1
  49.5 0.0 copy-done.2
  49.5 0.0 copy-done.6
  49.5 6.2 %final.1 = f32[5,1024,128]{2,1,0:T(8,128)} custom-call(f32[5,1024,128]{2,1,0:T(8,128)S(1)} %bitcast.14, f32[512,128]{1,0:T(8,128)S(1)} %bitcast.15, f32[5,32]{1,0:T(8,128)S(1)} %copy-done.4, f32[5,32]{1,0:T(8,128)S(1)} %copy-done.5, f32[5,32]{1,0:T(8,128)S(1)} %copy-done.6, f32[256,128]{1,0:T(8,128)S(1)} %bitcast.16, bf16[1024,256]{1,0:T(8,128)(2,1)S(1)} %copy-done.2), custom_call_target="tpu_custom_call" | custom-call | tf_op jit(solution)/shard_map/final/pallas_call | solution.py:317
  (1 shorter events, 0.0 us)
Async XLA Ops:
  0.0 1.7 %copy-start = (f32[5,16,32,256]{3,2,1,0:T(8,128)S(1)}, f32[5,16,32,256]{3,2,1,0:T(8,128)}, u32[]{:S(2)}) copy-start(f32[5,16,32,256]{3,2,1,0:T(8,128)} %param.6) | copy-start | bytes 7864324
  1.7 0.9 %copy-start.3 = (bf16[768,128]{1,0:T(8,128)(2,1)S(1)}, bf16[768,128]{1,0:T(8,128)(2,1)}, u32[]{:S(2)}) copy-start(bf16[768,128]{1,0:T(8,128)(2,1)} %constant.4.clone.w_ref) | copy-start | bytes 589828
  2.7 15.4 %copy-start.4 = (f32[5,32]{1,0:T(8,128)S(1)}, f32[5,32]{1,0:T(8,128)}, u32[]{:S(2)}) copy-start(f32[5,32]{1,0:T(8,128)} %lower_ref.3) | copy-start | bytes 1924
  2.7 15.5 %copy-start.5 = (f32[5,32]{1,0:T(8,128)S(1)}, f32[5,32]{1,0:T(8,128)}, u32[]{:S(2)}) copy-start(f32[5,32]{1,0:T(8,128)} %pivot_ref.3) | copy-start | bytes 1924
  3.9 45.5 %copy-start.1 = (f32[5,16,32,256]{3,2,1,0:T(8,128)S(1)}, f32[5,16,32,256]{3,2,1,0:T(8,128)}, u32[]{:S(2)}) copy-start(f32[5,16,32,256]{3,2,1,0:T(8,128)} %param.6) | copy-start | bytes 7864324
  3.9 45.5 %copy-start.2 = (bf16[1024,256]{1,0:T(8,128)(2,1)S(1)}, bf16[1024,256]{1,0:T(8,128)(2,1)}, u32[]{:S(2)}) copy-start(bf16[1024,256]{1,0:T(8,128)(2,1)} %constant.5.clone.w_ref) | copy-start | bytes 1572868
  4.0 45.5 %copy-start.6 = (f32[5,32]{1,0:T(8,128)S(1)}, f32[5,32]{1,0:T(8,128)}, u32[]{:S(2)}) copy-start(f32[5,32]{1,0:T(8,128)} %speed_ref.1) | copy-start | bytes 1924
  4.0 15.9 %collective-permute-start = (f32[5,8,128]{2,1,0:T(8,128)S(1)}, f32[5,8,128]{2,1,0:T(8,128)S(1)}, u32[]{:S(2)}, u32[]{:S(2)}) collective-permute-start(f32[5,8,128]{2,1,0:T(8,128)S(1)} %get-tuple-element.17), channel_id=1, source_target_pairs={{0,1},{1,2},{2,3},{3,4},{4,5},{5,6},{6,7},{7,8},{8,9},{9,10},{10,1... | collective-permute-start | bytes 61448 | tf_op jit(solution)/shard_map/ppermute | solution.py:287
  8.6 11.3 %collective-permute-start.1 = (f32[5,8,128]{2,1,0:T(8,128)S(1)}, f32[5,8,128]{2,1,0:T(8,128)S(1)}, u32[]{:S(2)}, u32[]{:S(2)}) collective-permute-start(f32[5,8,128]{2,1,0:T(8,128)S(1)} %get-tuple-element.18), channel_id=1, source_target_pairs={{1,0},{2,1},{3,2},{4,3},{5,4},{6,5},{7,6},{8,7},{9,8},{10,9},{11,1... | collective-permute-start | bytes 61448 | tf_op jit(solution)/shard_map/ppermute | solution.py:288

commit v2 on v1

--- a/solution.py
+++ b/solution.py
@@ -63,10 +63,22 @@
     return lax.broadcasted_iota(jnp.int32, shape, len(shape) - 2)
 
 
-def edge_kernel(c_ref, w_ref, left_ref, right_ref):
+def edge_kernel(c_hbm, w_hbm, lower_hbm, pivot_hbm, left_ref, right_ref, c_ref, rise_ref, fall_ref, unit_ref, w_ref, lower_ref, pivot_ref, sem):
+    small = [
+        pltpu.make_async_copy(a, b, sem.at[FIELDS + i])
+        for i, (a, b) in enumerate([(lower_hbm, lower_ref), (pivot_hbm, pivot_ref), (w_hbm, w_ref)])
+    ]
+    big = [pltpu.make_async_copy(c_hbm.at[f], c_ref.at[f], sem.at[f]) for f in range(FIELDS)]
+    for copy in small + big:
+        copy.start()
+    small[0].wait()
+    small[1].wait()
+    weights(lower_ref, pivot_ref, rise_ref, fall_ref, unit_ref)
+    small[2].wait()
     w = w_ref[...]
     lane32, lane = lanes((ROWS, 128)) % 16, lanes((8, 128)) // 32
     for f in range(FIELDS):
+        big[f].wait()
         tiles = c_ref[f].reshape(PLANES * 4, 2, 8, 128)
         rows = [tiles[:, h].reshape(PLANES * ROWS, 128) for h in range(2)]
         hi, lo = halves(jnp.concatenate(rows, axis=1))
@@ -92,42 +104,45 @@
     return jnp.concatenate([ref[f, pl.ds(row_of(j, h), PLANES, stride=64), :] for h in range(2)], 1)
 
 
+def full(ref, j, f):
+    v = ref[pl.ds(j * 8 + f, 8, stride=0), :]
+    return jnp.concatenate([jnp.concatenate([v, v], 0)] * 2, 1)
+
+
 def spread_rows(ref, out_ref):
     value = ref[...]
     for j in range(ROWS):
         out_ref[j * 8 : j * 8 + FIELDS, :] = jnp.broadcast_to(value[:, j : j + 1], (FIELDS, 128))
 
 
-def sums_kernel(c_ref, lower_ref, pivot_ref, out_ref, rise_ref, fall_ref, unit_ref):
-    low, piv = lower_ref[...], pivot_ref[...]
+def weights(lower_ref, pivot_ref, rise_ref, fall_ref, unit_ref):
+    low, piv = lower_ref[...], 1.0 / pivot_ref[...]
     wide = lambda v, j: jnp.broadcast_to(v[:, j : j + 1], (FIELDS, 128))
     entry = jnp.ones((FIELDS, 128), F32)
-    entries, inverse, spread = [], [], jnp.zeros((FIELDS, 128), F32)
-    for j in range(ROWS):
-        inverse.append(1.0 / wide(piv, j))
-        entries.append(entry)
-        spread = spread + entry * entry * inverse[j]
+    direct, spread = [], jnp.zeros((FIELDS, 128), F32)
+    for j in range(ROWS):
+        direct.append(entry * wide(piv, j))
+        spread = spread + entry * direct[j]
         entry = entry * wide(low, j)
     leave, first = None, None
     for j in reversed(range(ROWS)):
         l = wide(low, j)
         leave = l if leave is None else l * leave
-        first = entries[j] * inverse[j] if first is None else entries[j] * inverse[j] + l * first
+        first = direct[j] if first is None else direct[j] + l * first
         rise_ref[j * 8 : j * 8 + FIELDS, :] = leave
         fall_ref[j * 8 : j * 8 + FIELDS, :] = first
     unit_ref[0, :FIELDS, :] = entry
     unit_ref[1, :FIELDS, :] = spread
+
+
+def sums_kernel(c_ref, rise_ref, fall_ref, out_ref):
     for f in range(FIELDS):
         up = jnp.zeros((PLANES, CELLS), F32)
         down = jnp.zeros((PLANES, CELLS), F32)
         for j in range(ROWS):
             v = load_row(c_ref, f, j)
-            a = rise_ref[pl.ds(j * 8 + f, 8, stride=0), :]
-            b = fall_ref[pl.ds(j * 8 + f, 8, stride=0), :]
-            a = jnp.concatenate([jnp.concatenate([a, a], 0)] * 2, 1)
-            b = jnp.concatenate([jnp.concatenate([b, b], 0)] * 2, 1)
-            up = up + a * v
-            down = down + b * v
+            up = up + full(rise_ref, j, f) * v
+            down = down + full(fall_ref, j, f) * v
         for h in range(2):
             for q in range(2):
                 base = (16 * q + h) * 16 + f
@@ -196,7 +211,7 @@
         run = through_ref[d] * run + crest_ref[d]
 
 
-def final_kernel(c_ref, ret_ref, lower_ref, pivot_ref, speed_ref, ext_ref, w_ref, o_ref, low_ref, inv_ref, sp_ref, fe_ref, sc_ref, lhs_ref, res_ref, sem):
+def final_kernel(c_ref, ret_ref, lower_ref, pivot_ref, speed_ref, ext_ref, w_ref, o_ref, low_ref, inv_ref, sp_ref, fe_ref, fl_ref, sc_ref, lhs_ref, res_ref, sem):
     spread_rows(lower_ref, low_ref)
     spread_rows(speed_ref, sp_ref)
     value = 1.0 / pivot_ref[...]
@@ -223,41 +238,46 @@
         run = fe_ref[j * 8 : j * 8 + 8, :] + low_ref[j * 8 : j * 8 + 8, :] * run
         fe_ref[j * 8 : j * 8 + 8, :] = run * sp_ref[j * 8 : j * 8 + 8, :]
 
+    for j in range(ROWS):
+        hi, lo = halves(fe_ref[j * 8 : j * 8 + 8, :])
+        fe_ref[j * 8 : j * 8 + 8, :] = hi.astype(F32)
+        fl_ref[j * 8 : j * 8 + 8, :] = lo.astype(F32)
+
     mine = lanes((PLANES, 128)) % 16 == sublanes((PLANES, 128))
     w = w_ref[...]
 
-    def full(ref, j, f):
+    def carry(f, shift):
+        parts = [[ret_ref[pl.ds((16 * q + h) * 16 + f + shift, 8, stride=32), :] for h in range(2)] for q in range(2)]
+        return jnp.concatenate([jnp.concatenate(p, 1) for p in parts], 0)
+
+    def planes(ref, j, f):
         v = ref[pl.ds(j * 8 + f, 8, stride=0), :]
-        return jnp.concatenate([jnp.concatenate([v, v], 0)] * 2, 1)
-
+        return jnp.where(mine, jnp.concatenate([v, v], 0), 0.0).astype(BF16)
+
+    run = [carry(f, 0) for f in range(FIELDS)]
+    for j in range(ROWS):
+        for f in range(FIELDS):
+            now = load_row(c_ref, f, j) + run[f]
+            sc_ref[f, j * 16 : j * 16 + 16, :] = now * full(inv_ref, j, f)
+            run[f] = now * full(low_ref, j, f)
+    run = [carry(f, 8) for f in range(FIELDS)]
     copies = []
-    for f in range(FIELDS):
-        slot = f % 2
-
-        def carry(shift):
-            parts = [
-                [ret_ref[pl.ds((16 * q + h) * 16 + f + shift, 8, stride=32), :] for h in range(2)] for q in range(2)
-            ]
-            return jnp.concatenate([jnp.concatenate(p, 1) for p in parts], 0)
-
-        run = carry(0)
-        for j in range(ROWS):
-            run = load_row(c_ref, f, j) + run
-            sc_ref[slot, j * 16 : j * 16 + 16, :] = run * full(inv_ref, j, f)
-            run = run * full(low_ref, j, f)
-        run = carry(8)
-        for j in reversed(range(ROWS)):
-            run = sc_ref[slot, j * 16 : j * 16 + 16, :] + full(low_ref, j, f) * run
-            sc_ref[slot, j * 16 : j * 16 + 16, :] = run
-            hi, lo = halves(run * full(sp_ref, j, f))
-            e = fe_ref[pl.ds(j * 8 + f, 8, stride=0), :]
-            ehi, elo = halves(jnp.where(mine, jnp.concatenate([e, e], 0), 0.0))
-            lhs_ref[slot, j * 16 : j * 16 + 16, :] = jnp.concatenate([hi, lo, hi, ehi, elo], 1)
-        out = sc_ref[slot] + jnp.dot(lhs_ref[slot], w, preferred_element_type=F32)
-        for j in range(ROWS):
-            for h in range(2):
-                res_ref[f, pl.ds(row_of(j, h), PLANES, stride=64), :] = out[j * 16 : j * 16 + 16, 128 * h : 128 * h + 128]
-        copy = pltpu.make_async_copy(res_ref.at[f], o_ref.at[f], sem.at[f])
+    for t in reversed(range(4)):
+        for j in reversed(range(8 * t, 8 * t + 8)):
+            for f in range(FIELDS):
+                run[f] = sc_ref[f, j * 16 : j * 16 + 16, :] + full(low_ref, j, f) * run[f]
+                sc_ref[f, j * 16 : j * 16 + 16, :] = run[f]
+                hi, lo = halves(run[f] * full(sp_ref, j, f))
+                at = f * 128 + (j % 8) * 16
+                lhs_ref[t % 2, at : at + 16, :] = jnp.concatenate([hi, lo, hi, planes(fe_ref, j, f), planes(fl_ref, j, f)], 1)
+        out = jnp.dot(lhs_ref[t % 2], w, preferred_element_type=F32)
+        for f in range(FIELDS):
+            for s in range(8):
+                j, at = 8 * t + s, f * 128 + s * 16
+                value = out[at : at + 16] + sc_ref[f, j * 16 : j * 16 + 16, :]
+                for h in range(2):
+                    res_ref[t, pl.ds(f * 256 + h * 8 + s, PLANES, stride=16), :] = value[:, 128 * h : 128 * h + 128]
+        copy = pltpu.make_async_copy(res_ref.at[t].reshape(FIELDS * PLANES, 16, 128), o_ref.at[:, t], sem.at[t])
         copy.start()
         copies.append(copy)
     for copy in copies:
@@ -275,26 +295,33 @@
     stencil, edge = tables()
     sds = jax.ShapeDtypeStruct
     flat = cotangent.reshape(FIELDS, PLANES, 4, 8, 2, 128).transpose(0, 1, 2, 4, 3, 5).reshape(FIELDS, 1024, 128)
-    left, right = pl.pallas_call(
+    rows = sds((ROWS * 8, 128), F32)
+    left, right, cells, rise, fall, unit = pl.pallas_call(
         edge_kernel,
-        out_shape=[sds((FIELDS, 8, 128), F32)] * 2,
-        in_specs=[VM] * 2,
-        out_specs=[VM] * 2,
+        out_shape=[sds((FIELDS, 8, 128), F32)] * 2 + [sds((FIELDS, 1024, 128), F32), rows, rows, sds((2, 8, 128), F32)],
+        in_specs=[pl.BlockSpec(memory_space=pl.ANY)] * 4,
+        out_specs=[VM] * 6,
+        scratch_shapes=[
+            pltpu.VMEM((3 * CELLS, 128), BF16),
+            pltpu.VMEM((FIELDS, ROWS), F32),
+            pltpu.VMEM((FIELDS, ROWS), F32),
+            pltpu.SemaphoreType.DMA((FIELDS + 3,)),
+        ],
         compiler_params=params(),
         name="edge",
-    )(flat, jnp.asarray(edge))
+    )(flat, jnp.asarray(edge), lower, pivot)
     count = lax.axis_size("stream")
     from_left = lax.ppermute(right, "stream", [(i, (i + 1) % count) for i in range(count)])
     from_right = lax.ppermute(left, "stream", [((i + 1) % count, i) for i in range(count)])
-    main, rise, fall, unit = pl.pallas_call(
+    main = pl.pallas_call(
         sums_kernel,
-        out_shape=[sds((WALLS * 16, 128), F32), sds((ROWS * 8, 128), F32), sds((ROWS * 8, 128), F32), sds((2, 8, 128), F32)],
+        out_shape=sds((WALLS * 16, 128), F32),
         in_specs=[VM] * 3,
-        out_specs=[VM] * 4,
+        out_specs=VM,
         compiler_params=params(),
         cost_estimate=pl.CostEstimate(flops=4000000, bytes_accessed=2600000, transcendentals=0),
         name="sums",
-    )(flat, lower, pivot)
+    )(cells, rise, fall)
     send, ext = pl.pallas_call(
         merge_kernel,
         out_shape=[sds((WALLS, 16, 128), F32), sds((8, ROWS, 128), F32)],
@@ -316,19 +343,19 @@
     back = lax.all_to_all(carries, "wall", 0, 0, tiled=True)
     out = pl.pallas_call(
         final_kernel,
-        out_shape=sds((FIELDS, 1024, 128), F32),
+        out_shape=sds((FIELDS * PLANES, 4, 16, 128), F32),
         in_specs=[VM] * 7,
         out_specs=pl.BlockSpec(memory_space=pl.ANY),
-        scratch_shapes=[pltpu.VMEM((ROWS * 8, 128), F32)] * 4
+        scratch_shapes=[pltpu.VMEM((ROWS * 8, 128), F32)] * 5
         + [
-            pltpu.VMEM((2, ROWS * PLANES, CELLS), F32),
-            pltpu.VMEM((2, ROWS * PLANES, 1024), BF16),
-            pltpu.VMEM((FIELDS, 1024, 128), F32),
-            pltpu.SemaphoreType.DMA((FIELDS,)),
+            pltpu.VMEM((FIELDS, ROWS * PLANES, CELLS), F32),
+            pltpu.VMEM((2, FIELDS * PLANES * 8, 1024), BF16),
+            pltpu.VMEM((4, FIELDS * PLANES * 16, 128), F32),
+            pltpu.SemaphoreType.DMA((4,)),
         ],
         compiler_params=params(),
         name="final",
-    )(flat, back.reshape(WALLS * 16, 128), lower, pivot, speed, ext.reshape(8 * ROWS, 128), jnp.asarray(stencil))
+    )(cells, back.reshape(WALLS * 16, 128), lower, pivot, speed, ext.reshape(8 * ROWS, 128), jnp.asarray(stencil))
     return out.reshape(FIELDS, PLANES, 4, 2, 8, 128).transpose(0, 1, 2, 4, 3, 5).reshape(FIELDS, PLANES, ROWS, CELLS)
 
 

time: 55.9 us -> 58.4 us (1.045)
  local copies, waits for them, and re-layouts: 2.69 us -> 4.06 us
  Pallas kernels: 9.62 us -> 10.9 us
    unnamed x14 -> x16, local copies, waits for them, and re-layouts: 2.69 us -> 4.06 us
    pallas_call x3, Pallas kernels: 9.21 us -> 10.5 us  [the longest x1 5.1 us: local(): pl.pallas_call(final_kernel, out_shape=sds((FIELDS * PLANES, 4, 16, 128),...]
where the time goes in v2:
time: 58.4 us; the launch traced here: 58.1 us
  blocking collectives  29.1 us (50%)
  starting transfers between devices  13.9 us (24%)
  Pallas kernels  10.9 us (19%)
  local copies, waits for them, and re-layouts  4.06 us (7%)
    all_to_all x1, blocking collectives, local(): got = lax.all_to_all(send, 'wall', 0, 0, tiled=True)  16.7 us
    all_to_all x1, blocking collectives, local(): back = lax.all_to_all(carries, 'wall', 0, 0, tiled=True)  12.4 us
    ppermute x1, starting transfers between devices, local(): lax.ppermute(left, 'stream', [((i + 1) % count, i) for i in range(count)])  9.5 us
    pallas_call x1, Pallas kernels, local(): pl.pallas_call(final_kernel, out_shape=sds((FIELDS * PLANES, 4, 16, 128),...  5.1 us
    ppermute x1, starting transfers between devices, local(): lax.ppermute(right, 'stream', [(i, (i + 1) % count) for i in range(count)])  4.37 us
    unnamed x16, local copies, waits for them, and re-layouts  4.06 us
    pallas_call x1, Pallas kernels, local(): pl.pallas_call(edge_kernel, out_shape=[sds((FIELDS, 8, 128), F32)] * 2 +...  3.67 us
    pallas_call x1, Pallas kernels, local(): pl.pallas_call(sums_kernel, out_shape=sds((WALLS * 16, 128), F32), in_spe...  1.75 us
  transfers between devices with their start and end apart: 2, of which 0 were waited for; matrix products, arithmetic and copies ran while one was open for 0% of the time, Pallas kernels for 3%

profile of v2, /device:TPU:1, one launch (start us, length us, event | category | flops | bytes accessed | tf_op | source)
XLA Modules:
  0.0 58.1 jit_solution(4887824412639369009)
XLA Ops:
  0.0 0.0 copy-start
  0.0 1.7 %copy-done = f32[5,16,32,256]{3,2,1,0:T(8,128)S(1)} copy-done((f32[5,16,32,256]{3,2,1,0:T(8,128)S(1)}, f32[5,16,32,256]{3,2,1,0:T(8,128)}, u32[]{:S(2)}) %copy-start) | copy-done | bytes 2621464
  1.7 0.9 %copy-done.2 = bf16[768,128]{1,0:T(8,128)(2,1)S(1)} copy-done((bf16[768,128]{1,0:T(8,128)(2,1)S(1)}, bf16[768,128]{1,0:T(8,128)(2,1)}, u32[]{:S(2)}) %copy-start.2) | copy-done | bytes 196632
  2.7 0.7 %copy-done.3 = f32[5,32]{1,0:T(8,128)S(1)} copy-done((f32[5,32]{1,0:T(8,128)S(1)}, f32[5,32]{1,0:T(8,128)}, u32[]{:S(2)}) %copy-start.3) | copy-done | bytes 664
  3.4 0.7 %copy-done.5 = f32[5,32]{1,0:T(8,128)S(1)} copy-done((f32[5,32]{1,0:T(8,128)S(1)}, f32[5,32]{1,0:T(8,128)}, u32[]{:S(2)}) %copy-start.5) | copy-done | bytes 664
  4.0 3.7 %edge.1 = (f32[5,8,128]{2,1,0:T(8,128)S(1)}, f32[5,8,128]{2,1,0:T(8,128)S(1)}, f32[5,1024,128]{2,1,0:T(8,128)S(1)}, f32[256,128]{1,0:T(8,128)S(1)}, f32[256,128]{1,0:T(8,128)S(1)}, /*index=5*/f32[2,8,128]{2,1,0:T(8,128)S(1)}) custom-call(f32[5,1024,128]{2,1,0:T(8,128)S(1)} %bitcast.12, bf16[768,128]{1,0:T(8,128)(2,1)S(1)} %copy-done.2, ...), custom_call_target="tpu_custom_call" | custom-call | tf_op jit(solution)/shard_map/edge/pallas_call | solution.py:299
  7.7 4.4 %collective-permute-start = (f32[5,8,128]{2,1,0:T(8,128)S(1)}, f32[5,8,128]{2,1,0:T(8,128)S(1)}, u32[]{:S(2)}, u32[]{:S(2)}) collective-permute-start(f32[5,8,128]{2,1,0:T(8,128)S(1)} %get-tuple-element.17), channel_id=1, source_target_pairs={{0,1},{1,2},{2,3},{3,4},{4,5},{5,6},{6,7},{7,8},{8,9},{9,10},{10,1... | collective-permute-start | bytes 61448 | tf_op jit(solution)/shard_map/ppermute | solution.py:314
  12.1 9.5 %collective-permute-start.1 = (f32[5,8,128]{2,1,0:T(8,128)S(1)}, f32[5,8,128]{2,1,0:T(8,128)S(1)}, u32[]{:S(2)}, u32[]{:S(2)}) collective-permute-start(f32[5,8,128]{2,1,0:T(8,128)S(1)} %get-tuple-element.18), channel_id=1, source_target_pairs={{1,0},{2,1},{3,2},{4,3},{5,4},{6,5},{7,6},{8,7},{9,8},{10,9},{11,1... | collective-permute-start | bytes 61448 | tf_op jit(solution)/shard_map/ppermute | solution.py:315
  21.6 0.0 copy-start.1
  21.6 0.0 copy-start.4
  21.6 0.0 copy-start.6
  21.6 0.0 copy-start.7
  21.7 1.7 %sums.1.main_ref = f32[512,128]{1,0:T(8,128)S(1)} custom-call(f32[5,1024,128]{2,1,0:T(8,128)S(1)} %get-tuple-element.13.c_ref, f32[256,128]{1,0:T(8,128)S(1)} %get-tuple-element.14.rise_ref, f32[256,128]{1,0:T(8,128)S(1)} %get-tuple-element.15.fall_ref), custom_call_target="tpu_custom_call" | custom-call | flops 4000000 | bytes 2600000 | tf_op jit(solution)/shard_map/sums/pallas_call | solution.py:316
  23.4 0.0 collective-permute-done.left_ref
  23.4 0.0 collective-permute-done.1.right_ref
  23.4 0.2 merge.1
  23.6 16.7 %all_to_all.10.in_ref = f32[32,16,128]{2,1,0:T(8,128)S(1)} all-to-all(f32[32,16,128]{2,1,0:T(8,128)S(1)} %get-tuple-element.19), channel_id=1, replica_groups=mesh['wall'=32,'stream'=16] {'wall'}, dimensions={0} | all-to-all | bytes 524288 | tf_op jit(solution)/shard_map/all_to_all | solution.py:333
  40.3 0.2 carry.1
  40.6 12.4 %all_to_all.11 = f32[32,16,128]{2,1,0:T(8,128)S(1)} all-to-all(f32[32,16,128]{2,1,0:T(8,128)S(1)} %carry.1), channel_id=1, replica_groups=mesh['wall'=32,'stream'=16] {'wall'}, dimensions={0} | all-to-all | bytes 524288 | tf_op jit(solution)/shard_map/all_to_all | solution.py:343
  53.0 0.0 copy-done.1
  53.0 0.0 copy-done.4
  53.0 0.0 copy-done.6
  53.0 0.0 copy-done.7
  53.0 5.1 %final.1 = f32[80,4,16,128]{3,2,1,0:T(8,128)} custom-call(f32[5,1024,128]{2,1,0:T(8,128)S(1)} %get-tuple-element.13.c_ref, f32[512,128]{1,0:T(8,128)S(1)} %bitcast.13, f32[5,32]{1,0:T(8,128)S(1)} %copy-done.4, f32[5,32]{1,0:T(8,128)S(1)} %copy-done.6, f32[5,32]{1,0:T(8,128)S(1)} %copy-done.7, f32[256,128]{1,0:T(8,128)S(1)} %bitcast.14, ...), custom_call_target="tpu_custom_call" | custom-call | tf_op jit(solution)/shard_map/final/pallas_call | solution.py:344
  (3 shorter events, 0.0 us)
Async XLA Ops:
  0.0 1.7 %copy-start = (f32[5,16,32,256]{3,2,1,0:T(8,128)S(1)}, f32[5,16,32,256]{3,2,1,0:T(8,128)}, u32[]{:S(2)}) copy-start(f32[5,16,32,256]{3,2,1,0:T(8,128)} %param.6) | copy-start | bytes 7864324
  1.7 0.9 %copy-start.2 = (bf16[768,128]{1,0:T(8,128)(2,1)S(1)}, bf16[768,128]{1,0:T(8,128)(2,1)}, u32[]{:S(2)}) copy-start(bf16[768,128]{1,0:T(8,128)(2,1)} %constant.4.clone.w_hbm) | copy-start | bytes 589828
  2.7 0.7 %copy-start.3 = (f32[5,32]{1,0:T(8,128)S(1)}, f32[5,32]{1,0:T(8,128)}, u32[]{:S(2)}) copy-start(f32[5,32]{1,0:T(8,128)} %lower_ref.1) | copy-start | bytes 1924
  3.4 0.7 %copy-start.5 = (f32[5,32]{1,0:T(8,128)S(1)}, f32[5,32]{1,0:T(8,128)}, u32[]{:S(2)}) copy-start(f32[5,32]{1,0:T(8,128)} %pivot_ref.1) | copy-start | bytes 1924
  7.7 15.7 %collective-permute-start = (f32[5,8,128]{2,1,0:T(8,128)S(1)}, f32[5,8,128]{2,1,0:T(8,128)S(1)}, u32[]{:S(2)}, u32[]{:S(2)}) collective-permute-start(f32[5,8,128]{2,1,0:T(8,128)S(1)} %get-tuple-element.17), channel_id=1, source_target_pairs={{0,1},{1,2},{2,3},{3,4},{4,5},{5,6},{6,7},{7,8},{8,9},{9,10},{10,1... | collective-permute-start | bytes 61448 | tf_op jit(solution)/shard_map/ppermute | solution.py:314
  12.1 11.3 %collective-permute-start.1 = (f32[5,8,128]{2,1,0:T(8,128)S(1)}, f32[5,8,128]{2,1,0:T(8,128)S(1)}, u32[]{:S(2)}, u32[]{:S(2)}) collective-permute-start(f32[5,8,128]{2,1,0:T(8,128)S(1)} %get-tuple-element.18), channel_id=1, source_target_pairs={{1,0},{2,1},{3,2},{4,3},{5,4},{6,5},{7,6},{8,7},{9,8},{10,9},{11,1... | collective-permute-start | bytes 61448 | tf_op jit(solution)/shard_map/ppermute | solution.py:315
  21.6 31.4 %copy-start.1 = (bf16[1024,256]{1,0:T(8,128)(2,1)S(1)}, bf16[1024,256]{1,0:T(8,128)(2,1)}, u32[]{:S(2)}) copy-start(bf16[1024,256]{1,0:T(8,128)(2,1)} %constant.5.clone.w_ref) | copy-start | bytes 1572868
  21.6 31.4 %copy-start.4 = (f32[5,32]{1,0:T(8,128)S(1)}, f32[5,32]{1,0:T(8,128)}, u32[]{:S(2)}) copy-start(f32[5,32]{1,0:T(8,128)} %lower_ref.1) | copy-start | bytes 1924
  21.6 31.4 %copy-start.6 = (f32[5,32]{1,0:T(8,128)S(1)}, f32[5,32]{1,0:T(8,128)}, u32[]{:S(2)}) copy-start(f32[5,32]{1,0:T(8,128)} %pivot_ref.1) | copy-start | bytes 1924
  21.6 31.4 %copy-start.7 = (f32[5,32]{1,0:T(8,128)S(1)}, f32[5,32]{1,0:T(8,128)}, u32[]{:S(2)}) copy-start(f32[5,32]{1,0:T(8,128)} %speed_ref.1) | copy-start | bytes 1924

commit v3 on v2

--- a/solution.py
+++ b/solution.py
@@ -65,43 +65,49 @@
 
 def edge_kernel(c_hbm, w_hbm, lower_hbm, pivot_hbm, left_ref, right_ref, c_ref, rise_ref, fall_ref, unit_ref, w_ref, lower_ref, pivot_ref, sem):
     small = [
-        pltpu.make_async_copy(a, b, sem.at[FIELDS + i])
+        pltpu.make_async_copy(a, b, sem.at[i])
         for i, (a, b) in enumerate([(lower_hbm, lower_ref), (pivot_hbm, pivot_ref), (w_hbm, w_ref)])
     ]
-    big = [pltpu.make_async_copy(c_hbm.at[f], c_ref.at[f], sem.at[f]) for f in range(FIELDS)]
-    for copy in small + big:
+    big = [
+        [
+            pltpu.make_async_copy(c_hbm.at[f, :, t, h], c_ref.at[f, t, h], sem.at[3 + (f * 4 + t) * 2 + h])
+            for t in range(4)
+            for h in range(2)
+        ]
+        for f in range(FIELDS)
+    ]
+    for copy in small + sum(big, []):
         copy.start()
     small[0].wait()
     small[1].wait()
     weights(lower_ref, pivot_ref, rise_ref, fall_ref, unit_ref)
     small[2].wait()
     w = w_ref[...]
-    lane32, lane = lanes((ROWS, 128)) % 16, lanes((8, 128)) // 32
+    plane, lane = lanes((8, 128)) % 16, lanes((8, 128)) // 32
     for f in range(FIELDS):
-        big[f].wait()
-        tiles = c_ref[f].reshape(PLANES * 4, 2, 8, 128)
-        rows = [tiles[:, h].reshape(PLANES * ROWS, 128) for h in range(2)]
+        for copy in big[f]:
+            copy.wait()
+        rows = [c_ref[f, :, h].reshape(PLANES * ROWS, 128) for h in range(2)]
         hi, lo = halves(jnp.concatenate(rows, axis=1))
         sums = jnp.dot(jnp.concatenate([hi, lo, hi], axis=1), w, preferred_element_type=F32)
-        own = sums[:ROWS]
-        for p in range(1, PLANES):
-            own = jnp.where(lane32 == p, sums[p * ROWS : (p + 1) * ROWS], own)
-        left = own[:8]
-        right = pltpu.roll(own[:8], 96, 1)
+        own = []
+        for t in range(4):
+            part = sums[t * 128 : t * 128 + 8]
+            for p in range(1, PLANES):
+                part = jnp.where(plane == p, sums[t * 128 + p * 8 : t * 128 + p * 8 + 8], part)
+            own.append(part)
+        left = own[0]
+        right = pltpu.roll(own[0], 96, 1)
         for q in range(1, 4):
-            part = own[8 * q : 8 * q + 8]
+            part = own[q]
             left = jnp.where(lane == q, pltpu.roll(part, 32 * q, 1), left)
             right = jnp.where(lane == q, pltpu.roll(part, (32 * q + 96) % 128, 1) if q != 1 else part, right)
         left_ref[f] = left
         right_ref[f] = right
 
 
-def row_of(j, h):
-    return (j // 8) * 16 + h * 8 + j % 8
-
-
-def load_row(ref, f, j):
-    return jnp.concatenate([ref[f, pl.ds(row_of(j, h), PLANES, stride=64), :] for h in range(2)], 1)
+def load_row(ref, f, t, s):
+    return jnp.concatenate([ref[f, pl.ds(t * 256 + h * 128 + s, PLANES, stride=8), :] for h in range(2)], 1)
 
 
 def full(ref, j, f):
@@ -140,14 +146,14 @@
         up = jnp.zeros((PLANES, CELLS), F32)
         down = jnp.zeros((PLANES, CELLS), F32)
         for j in range(ROWS):
-            v = load_row(c_ref, f, j)
+            v = load_row(c_ref, f, j // 8, j % 8)
             up = up + full(rise_ref, j, f) * v
             down = down + full(fall_ref, j, f) * v
         for h in range(2):
             for q in range(2):
-                base = (16 * q + h) * 16 + f
-                out_ref[pl.ds(base, 8, stride=32), :] = up[8 * q : 8 * q + 8, 128 * h : 128 * h + 128]
-                out_ref[pl.ds(base + 8, 8, stride=32), :] = down[8 * q : 8 * q + 8, 128 * h : 128 * h + 128]
+                base = (16 * h + 8 * q) * 16 + f
+                out_ref[pl.ds(base, 8, stride=16), :] = up[8 * q : 8 * q + 8, 128 * h : 128 * h + 128]
+                out_ref[pl.ds(base + 8, 8, stride=16), :] = down[8 * q : 8 * q + 8, 128 * h : 128 * h + 128]
 
 
 def merge_kernel(main_ref, rise_ref, fall_ref, unit_ref, left_ref, right_ref, out_ref, ext_ref):
@@ -162,13 +168,11 @@
             l = pltpu.roll(from_left, (128 - 32 * q + 32) % 128, 1) if q != 1 else from_left
             v = jnp.where(lane < 32, r, l)
             v = jnp.where(lane < 64, v, pltpu.roll(v, 64, 1))
-            ext_ref[f, 8 * q : 8 * q + 8, :] = v
+            ext_ref[pl.ds(64 * q + f, 8, stride=8), :] = v
             up = up + rise_ref[pl.ds(64 * q + f, 8, stride=8), :] * v
             down = down + fall_ref[pl.ds(64 * q + f, 8, stride=8), :] * v
         ups.append(jnp.sum(up, axis=0, keepdims=True))
         downs.append(jnp.sum(down, axis=0, keepdims=True))
-    for f in range(FIELDS, 8):
-        ext_ref[f] = jnp.zeros((ROWS, 128), F32)
     row = sublanes((FIELDS, 128))
     lane5 = lanes((FIELDS, 128))
     coef = jnp.where(lane5 == 64 + row, unit_ref[0, :FIELDS, :], 0.0)
@@ -230,7 +234,7 @@
 
     run = unpack(ret_ref[0:8, :])
     for j in range(ROWS):
-        run = ext_ref[pl.ds(j, 8, stride=ROWS), :] + run
+        run = ext_ref[j * 8 : j * 8 + 8, :] + run
         fe_ref[j * 8 : j * 8 + 8, :] = run * inv_ref[j * 8 : j * 8 + 8, :]
         run = run * low_ref[j * 8 : j * 8 + 8, :]
     run = unpack(ret_ref[8:16, :])
@@ -247,19 +251,23 @@
     w = w_ref[...]
 
     def carry(f, shift):
-        parts = [[ret_ref[pl.ds((16 * q + h) * 16 + f + shift, 8, stride=32), :] for h in range(2)] for q in range(2)]
+        parts = [[ret_ref[pl.ds((16 * h + 8 * q) * 16 + f + shift, 8, stride=16), :] for h in range(2)] for q in range(2)]
         return jnp.concatenate([jnp.concatenate(p, 1) for p in parts], 0)
 
     def planes(ref, j, f):
         v = ref[pl.ds(j * 8 + f, 8, stride=0), :]
         return jnp.where(mine, jnp.concatenate([v, v], 0), 0.0).astype(BF16)
 
-    run = [carry(f, 0) for f in range(FIELDS)]
-    for j in range(ROWS):
-        for f in range(FIELDS):
-            now = load_row(c_ref, f, j) + run[f]
-            sc_ref[f, j * 16 : j * 16 + 16, :] = now * full(inv_ref, j, f)
-            run[f] = now * full(low_ref, j, f)
+    def rise(t, run):
+        run = list(run)
+        for s in range(8):
+            for f in range(FIELDS):
+                now = load_row(c_ref, f, t, s) + run[f]
+                sc_ref[f, pl.ds(pl.multiple_of(t * 128, 128) + s * 16, 16), :] = now * full(inv_ref, t * 8 + s, f)
+                run[f] = now * full(low_ref, t * 8 + s, f)
+        return tuple(run)
+
+    lax.fori_loop(0, 4, rise, tuple(carry(f, 0) for f in range(FIELDS)))
     run = [carry(f, 8) for f in range(FIELDS)]
     copies = []
     for t in reversed(range(4)):
@@ -276,10 +284,11 @@
                 j, at = 8 * t + s, f * 128 + s * 16
                 value = out[at : at + 16] + sc_ref[f, j * 16 : j * 16 + 16, :]
                 for h in range(2):
-                    res_ref[t, pl.ds(f * 256 + h * 8 + s, PLANES, stride=16), :] = value[:, 128 * h : 128 * h + 128]
-        copy = pltpu.make_async_copy(res_ref.at[t].reshape(FIELDS * PLANES, 16, 128), o_ref.at[:, t], sem.at[t])
-        copy.start()
-        copies.append(copy)
+                    res_ref[t, h, pl.ds(f * 128 + s, PLANES, stride=8), :] = value[:, 128 * h : 128 * h + 128]
+        for h in range(2):
+            source = res_ref.at[t, h].reshape(FIELDS * PLANES, 8, 128)
+            copies.append(pltpu.make_async_copy(source, o_ref.at[:, t, h], sem.at[2 * t + h]))
+            copies[-1].start()
     for copy in copies:
         copy.wait()
 
@@ -294,22 +303,23 @@
 def local(cotangent, lower, pivot, speed):
     stencil, edge = tables()
     sds = jax.ShapeDtypeStruct
-    flat = cotangent.reshape(FIELDS, PLANES, 4, 8, 2, 128).transpose(0, 1, 2, 4, 3, 5).reshape(FIELDS, 1024, 128)
+    flat = cotangent.reshape(FIELDS, PLANES, 4, 8, 2, 128).transpose(0, 1, 2, 4, 3, 5)
     rows = sds((ROWS * 8, 128), F32)
     left, right, cells, rise, fall, unit = pl.pallas_call(
         edge_kernel,
-        out_shape=[sds((FIELDS, 8, 128), F32)] * 2 + [sds((FIELDS, 1024, 128), F32), rows, rows, sds((2, 8, 128), F32)],
-        in_specs=[pl.BlockSpec(memory_space=pl.ANY)] * 4,
+        out_shape=[sds((FIELDS, 8, 128), F32)] * 2 + [sds((FIELDS, 4, 2, PLANES, 8, 128), F32), rows, rows, sds((2, 8, 128), F32)],
+        in_specs=[pl.BlockSpec(memory_space=pltpu.HBM)] * 4,
         out_specs=[VM] * 6,
         scratch_shapes=[
             pltpu.VMEM((3 * CELLS, 128), BF16),
             pltpu.VMEM((FIELDS, ROWS), F32),
             pltpu.VMEM((FIELDS, ROWS), F32),
-            pltpu.SemaphoreType.DMA((FIELDS + 3,)),
+            pltpu.SemaphoreType.DMA((8 * FIELDS + 3,)),
         ],
         compiler_params=params(),
         name="edge",
-    )(flat, jnp.asarray(edge), lower, pivot)
+    )(*[pltpu.with_memory_space_constraint(v, pltpu.HBM) for v in (flat, jnp.asarray(edge), lower, pivot)])
+    cells = cells.reshape(FIELDS, 1024, 128)
     count = lax.axis_size("stream")
     from_left = lax.ppermute(right, "stream", [(i, (i + 1) % count) for i in range(count)])
     from_right = lax.ppermute(left, "stream", [((i + 1) % count, i) for i in range(count)])
@@ -324,7 +334,7 @@
     )(cells, rise, fall)
     send, ext = pl.pallas_call(
         merge_kernel,
-        out_shape=[sds((WALLS, 16, 128), F32), sds((8, ROWS, 128), F32)],
+        out_shape=[sds((WALLS, 16, 128), F32), rows],
         in_specs=[VM] * 6,
         out_specs=[VM] * 2,
         compiler_params=params(),
@@ -343,19 +353,19 @@
     back = lax.all_to_all(carries, "wall", 0, 0, tiled=True)
     out = pl.pallas_call(
         final_kernel,
-        out_shape=sds((FIELDS * PLANES, 4, 16, 128), F32),
+        out_shape=sds((FIELDS * PLANES, 4, 2, 8, 128), F32),
         in_specs=[VM] * 7,
         out_specs=pl.BlockSpec(memory_space=pl.ANY),
         scratch_shapes=[pltpu.VMEM((ROWS * 8, 128), F32)] * 5
         + [
             pltpu.VMEM((FIELDS, ROWS * PLANES, CELLS), F32),
             pltpu.VMEM((2, FIELDS * PLANES * 8, 1024), BF16),
-            pltpu.VMEM((4, FIELDS * PLANES * 16, 128), F32),
-            pltpu.SemaphoreType.DMA((4,)),
+            pltpu.VMEM((4, 2, FIELDS * PLANES * 8, 128), F32),
+            pltpu.SemaphoreType.DMA((8,)),
         ],
         compiler_params=params(),
         name="final",
-    )(cells, back.reshape(WALLS * 16, 128), lower, pivot, speed, ext.reshape(8 * ROWS, 128), jnp.asarray(stencil))
+    )(cells, back.reshape(WALLS * 16, 128), lower, pivot, speed, ext, jnp.asarray(stencil))
     return out.reshape(FIELDS, PLANES, 4, 2, 8, 128).transpose(0, 1, 2, 4, 3, 5).reshape(FIELDS, PLANES, ROWS, CELLS)
 
 

time: 58.4 us -> 53.8 us (0.921)
  local copies, waits for them, and re-layouts: 4.06 us -> 0.03 us
  Pallas kernels: 10.9 us -> 9.65 us
  blocking collectives: 29.1 us -> 29.7 us
    unnamed x16 -> x8, local copies, waits for them, and re-layouts: 4.06 us -> 0.03 us
    pallas_call x1, Pallas kernels: 1.75 us -> 0.64 us  [local(): pl.pallas_call(sums_kernel, out_shape=sds((WALLS * 16, 128), F32), in_spe...]
    pallas_call x2, Pallas kernels: 5.3 us -> 4.26 us  [the longest x1 4.06 us: local(): pl.pallas_call(final_kernel, out_shape=sds((FIELDS * PLANES, 4, 2, 8, 128...]
    pallas_call x1, Pallas kernels: 3.67 us -> 4.54 us  [local(): pl.pallas_call(edge_kernel, out_shape=[sds((FIELDS, 8, 128), F32)] * 2 +...]
  transfers between devices with their start and end apart: 2 -> 2, of which waited for: 0 -> 1; matrix products, arithmetic and copies ran while one was open for 0% -> 0% of each run, Pallas kernels for 3% -> 1%
where the time goes in v3:
time: 53.8 us; the launch traced here: 53.5 us
  blocking collectives  29.7 us (55%)
  starting transfers between devices  13.9 us (26%)
  Pallas kernels  9.65 us (18%)
    all_to_all x1, blocking collectives, local(): got = lax.all_to_all(send, 'wall', 0, 0, tiled=True)  17.3 us
    all_to_all x1, blocking collectives, local(): back = lax.all_to_all(carries, 'wall', 0, 0, tiled=True)  12.4 us
    ppermute x1, starting transfers between devices, local(): lax.ppermute(left, 'stream', [((i + 1) % count, i) for i in range(count)])  9.5 us
    pallas_call x1, Pallas kernels, local(): pl.pallas_call(edge_kernel, out_shape=[sds((FIELDS, 8, 128), F32)] * 2 +...  4.54 us
    ppermute x1, starting transfers between devices, local(): lax.ppermute(right, 'stream', [(i, (i + 1) % count) for i in range(count)])  4.36 us
    pallas_call x1, Pallas kernels, local(): pl.pallas_call(final_kernel, out_shape=sds((FIELDS * PLANES, 4, 2, 8, 128...  4.06 us
  transfers between devices with their start and end apart: 2, of which 1 were waited for; matrix products, arithmetic and copies ran while one was open for 0% of the time, Pallas kernels for 1%

profile of v3, /device:TPU:1, one launch (start us, length us, event | category | flops | bytes accessed | tf_op | source)
XLA Modules:
  0.0 53.5 jit_solution(8011697235598129279)
XLA Ops:
  0.0 4.5 %edge.1 = (f32[5,8,128]{2,1,0:T(8,128)S(1)}, f32[5,8,128]{2,1,0:T(8,128)S(1)}, f32[5,4,2,16,8,128]{5,4,3,2,1,0:T(8,128)S(1)}, f32[256,128]{1,0:T(8,128)S(1)}, f3...) custom-call(f32[5,16,4,2,8,128]{5,4,3,2,1,0:T(8,128)} %bitcast.13, bf16[768,128]{1,0:T(8,128)(2,1)} %constant.4.clone.w_hbm, ...), custom_call_target="tpu_custom_call" | custom-call | tf_op jit(solution)/shard_map/edge/pallas_call | solution.py:308
  4.5 4.4 %collective-permute-start = (f32[5,8,128]{2,1,0:T(8,128)S(1)}, f32[5,8,128]{2,1,0:T(8,128)S(1)}, u32[]{:S(2)}, u32[]{:S(2)}) collective-permute-start(f32[5,8,128]{2,1,0:T(8,128)S(1)} %get-tuple-element.17), channel_id=1, source_target_pairs={{0,1},{1,2},{2,3},{3,4},{4,5},{5,6},{6,7},{7,8},{8,9},{9,10},{10,1... | collective-permute-start | bytes 61448 | tf_op jit(solution)/shard_map/ppermute | solution.py:324
  8.9 9.5 %collective-permute-start.1 = (f32[5,8,128]{2,1,0:T(8,128)S(1)}, f32[5,8,128]{2,1,0:T(8,128)S(1)}, u32[]{:S(2)}, u32[]{:S(2)}) collective-permute-start(f32[5,8,128]{2,1,0:T(8,128)S(1)} %get-tuple-element.18), channel_id=1, source_target_pairs={{1,0},{2,1},{3,2},{4,3},{5,4},{6,5},{7,6},{8,7},{9,8},{10,9},{11,1... | collective-permute-start | bytes 61448 | tf_op jit(solution)/shard_map/ppermute | solution.py:325
  18.4 0.0 copy-start
  18.4 0.0 copy-start.1
  18.4 0.0 copy-start.2
  18.5 0.0 copy-start.3
  18.5 0.6 %sums.1.main_ref = f32[512,128]{1,0:T(8,128)S(1)} custom-call(f32[5,1024,128]{2,1,0:T(8,128)S(1)} %bitcast.10, f32[256,128]{1,0:T(8,128)S(1)} %get-tuple-element.14.rise_ref, f32[256,128]{1,0:T(8,128)S(1)} %get-tuple-element.15.fall_ref), custom_call_target="tpu_custom_call" | custom-call | flops 4000000 | bytes 2600000 | tf_op jit(solution)/shard_map/sums/pallas_call | solution.py:326
  19.1 0.0 collective-permute-done.left_ref
  19.1 0.2 collective-permute-done.1.right_ref
  19.3 0.2 merge.1
  19.5 17.3 %all_to_all.10.in_ref = f32[32,16,128]{2,1,0:T(8,128)S(1)} all-to-all(f32[32,16,128]{2,1,0:T(8,128)S(1)} %get-tuple-element.19), channel_id=1, replica_groups=mesh['wall'=32,'stream'=16] {'wall'}, dimensions={0} | all-to-all | bytes 524288 | tf_op jit(solution)/shard_map/all_to_all | solution.py:343
  36.8 0.2 carry.1
  37.0 12.4 %all_to_all.11 = f32[32,16,128]{2,1,0:T(8,128)S(1)} all-to-all(f32[32,16,128]{2,1,0:T(8,128)S(1)} %carry.1), channel_id=1, replica_groups=mesh['wall'=32,'stream'=16] {'wall'}, dimensions={0} | all-to-all | bytes 524288 | tf_op jit(solution)/shard_map/all_to_all | solution.py:353
  49.5 0.0 copy-done
  49.5 0.0 copy-done.1
  49.5 0.0 copy-done.2
  49.5 0.0 copy-done.3
  49.5 4.1 %final.1 = f32[80,4,2,8,128]{4,3,2,1,0:T(8,128)} custom-call(f32[5,1024,128]{2,1,0:T(8,128)S(1)} %bitcast.11, f32[512,128]{1,0:T(8,128)S(1)} %bitcast.12, f32[5,32]{1,0:T(8,128)S(1)} %copy-done.1, f32[5,32]{1,0:T(8,128)S(1)} %copy-done.2, f32[5,32]{1,0:T(8,128)S(1)} %copy-done.3, f32[256,128]{1,0:T(8,128)S(1)} %get-tuple-element.20.ext_ref, ...), custom_call_target="tpu_custom_call" | custom-call | tf_op jit(solution)/shard_map/final/pallas_call | solution.py:354
Async XLA Ops:
  4.5 14.6 %collective-permute-start = (f32[5,8,128]{2,1,0:T(8,128)S(1)}, f32[5,8,128]{2,1,0:T(8,128)S(1)}, u32[]{:S(2)}, u32[]{:S(2)}) collective-permute-start(f32[5,8,128]{2,1,0:T(8,128)S(1)} %get-tuple-element.17), channel_id=1, source_target_pairs={{0,1},{1,2},{2,3},{3,4},{4,5},{5,6},{6,7},{7,8},{8,9},{9,10},{10,1... | collective-permute-start | bytes 61448 | tf_op jit(solution)/shard_map/ppermute | solution.py:324
  8.9 10.4 %collective-permute-start.1 = (f32[5,8,128]{2,1,0:T(8,128)S(1)}, f32[5,8,128]{2,1,0:T(8,128)S(1)}, u32[]{:S(2)}, u32[]{:S(2)}) collective-permute-start(f32[5,8,128]{2,1,0:T(8,128)S(1)} %get-tuple-element.18), channel_id=1, source_target_pairs={{1,0},{2,1},{3,2},{4,3},{5,4},{6,5},{7,6},{8,7},{9,8},{10,9},{11,1... | collective-permute-start | bytes 61448 | tf_op jit(solution)/shard_map/ppermute | solution.py:325
  18.4 31.0 %copy-start = (bf16[1024,256]{1,0:T(8,128)(2,1)S(1)}, bf16[1024,256]{1,0:T(8,128)(2,1)}, u32[]{:S(2)}) copy-start(bf16[1024,256]{1,0:T(8,128)(2,1)} %constant.5.clone.w_ref) | copy-start | bytes 1572868
  18.4 31.0 %copy-start.1 = (f32[5,32]{1,0:T(8,128)S(1)}, f32[5,32]{1,0:T(8,128)}, u32[]{:S(2)}) copy-start(f32[5,32]{1,0:T(8,128)} %lower_ref.1) | copy-start | bytes 1924
  18.4 31.0 %copy-start.2 = (f32[5,32]{1,0:T(8,128)S(1)}, f32[5,32]{1,0:T(8,128)}, u32[]{:S(2)}) copy-start(f32[5,32]{1,0:T(8,128)} %pivot_ref.1) | copy-start | bytes 1924
  18.5 31.0 %copy-start.3 = (f32[5,32]{1,0:T(8,128)S(1)}, f32[5,32]{1,0:T(8,128)}, u32[]{:S(2)}) copy-start(f32[5,32]{1,0:T(8,128)} %speed_ref.1) | copy-start | bytes 1924

commit v4 on v3

--- a/solution.py
+++ b/solution.py
@@ -45,7 +45,8 @@
     edge[0, 1] = 1.0
     edge[:, 2] = dec(CELLS - 1 - x)
     edge[CELLS - 1, 3] = 1.0
-    edge = np.concatenate([np.repeat(edge, PLANES, axis=1), np.zeros((CELLS, 64))], axis=1)
+    edge = np.concatenate([edge[:64], edge[CELLS - 64 :]], axis=0)
+    edge = np.concatenate([np.repeat(edge, PLANES, axis=1), np.zeros((128, 64))], axis=1)
     ghi, glo = split_np(edge)
     return stencil, np.concatenate([ghi, ghi, glo], axis=0)
 
@@ -87,8 +88,8 @@
     for f in range(FIELDS):
         for copy in big[f]:
             copy.wait()
-        rows = [c_ref[f, :, h].reshape(PLANES * ROWS, 128) for h in range(2)]
-        hi, lo = halves(jnp.concatenate(rows, axis=1))
+        ends = [c_ref[f, :, h].reshape(PLANES * ROWS, 128) for h in range(2)]
+        hi, lo = halves(jnp.where(lanes((PLANES * ROWS, 128)) < 64, ends[0], ends[1]))
         sums = jnp.dot(jnp.concatenate([hi, lo, hi], axis=1), w, preferred_element_type=F32)
         own = []
         for t in range(4):
@@ -115,8 +116,7 @@
     return jnp.concatenate([jnp.concatenate([v, v], 0)] * 2, 1)
 
 
-def spread_rows(ref, out_ref):
-    value = ref[...]
+def spread_rows(value, out_ref):
     for j in range(ROWS):
         out_ref[j * 8 : j * 8 + FIELDS, :] = jnp.broadcast_to(value[:, j : j + 1], (FIELDS, 128))
 
@@ -141,7 +141,10 @@
     unit_ref[1, :FIELDS, :] = spread
 
 
-def sums_kernel(c_ref, rise_ref, fall_ref, out_ref):
+def sums_kernel(c_ref, rise_ref, fall_ref, lower_ref, pivot_ref, speed_ref, out_ref, low_ref, inv_ref, sp_ref):
+    spread_rows(lower_ref[...], low_ref)
+    spread_rows(1.0 / pivot_ref[...], inv_ref)
+    spread_rows(speed_ref[...], sp_ref)
     for f in range(FIELDS):
         up = jnp.zeros((PLANES, CELLS), F32)
         down = jnp.zeros((PLANES, CELLS), F32)
@@ -191,7 +194,8 @@
         out_ref[k, 8:, :] = jnp.where(sub < 5, main_ref[16 * k + 8 : 16 * k + 16, :], tail_down)
 
 
-def carry_kernel(in_ref, out_ref, through_ref, crest_ref):
+def carry_kernel(in_ref, out_ref, seam_ref, through_ref, crest_ref):
+    me = lax.axis_index("wall")
     sub, lane = sublanes((8, 128)), lanes((8, 128))
     low_field = jnp.where(sub < 5, sub, 2 * (sub - 5))
     high_field = jnp.where(sub < 5, sub, jnp.where(sub < 7, 2 * (sub - 5) + 1, 4))
@@ -201,26 +205,28 @@
         hi = jnp.sum(jnp.where(lane == at + high_field, row, 0.0), axis=1, keepdims=True)
         return jnp.where(lane < 64, lo, hi)
 
-    run = jnp.zeros((8, 128), F32)
+    run, mine = jnp.zeros((8, 128), F32), jnp.zeros((8, 128), F32)
     for d in range(WALLS):
         row = jnp.broadcast_to(in_ref[d, 7:8, :], (8, 128))
         through, spread = pick(row, 64), pick(row, 72)
         through_ref[d] = through
-        out_ref[d, :8, :] = run
+        out_ref[12 * d : 12 * d + 5, :] = run[:5]
+        mine = jnp.where(me == d, run, mine)
         crest_ref[d] = in_ref[d, 8:, :] + spread * run
         run = through * run + in_ref[d, :8, :]
-    run = jnp.zeros((8, 128), F32)
+    seam_ref[0] = mine
+    run, mine = jnp.zeros((8, 128), F32), jnp.zeros((8, 128), F32)
     for d in reversed(range(WALLS)):
-        out_ref[d, 8:, :] = run
+        out_ref[12 * d + 5 : 12 * d + 10, :] = run[:5]
+        out_ref[12 * d + 10 : 12 * d + 12, :] = jnp.zeros((2, 128), F32)
+        mine = jnp.where(me == d, run, mine)
         run = through_ref[d] * run + crest_ref[d]
-
-
-def final_kernel(c_ref, ret_ref, lower_ref, pivot_ref, speed_ref, ext_ref, w_ref, o_ref, low_ref, inv_ref, sp_ref, fe_ref, fl_ref, sc_ref, lhs_ref, res_ref, sem):
-    spread_rows(lower_ref, low_ref)
-    spread_rows(speed_ref, sp_ref)
-    value = 1.0 / pivot_ref[...]
-    for j in range(ROWS):
-        inv_ref[j * 8 : j * 8 + FIELDS, :] = jnp.broadcast_to(value[:, j : j + 1], (FIELDS, 128))
+    seam_ref[1] = mine
+
+
+def final_kernel(
+    c_ref, ret_ref, seam_ref, low_ref, inv_ref, sp_ref, ext_ref, w_ref, o_ref, fe_ref, fl_ref, sc_ref, lhs_ref, res_ref, sem
+):
     sub, lane = sublanes((8, 128)), lanes((8, 128))
 
     def unpack(tile):
@@ -232,12 +238,12 @@
             out = jnp.where(sub == f, rows[f], out)
         return jnp.where(sub < FIELDS, out, 0.0)
 
-    run = unpack(ret_ref[0:8, :])
+    run = unpack(seam_ref[0])
     for j in range(ROWS):
         run = ext_ref[j * 8 : j * 8 + 8, :] + run
         fe_ref[j * 8 : j * 8 + 8, :] = run * inv_ref[j * 8 : j * 8 + 8, :]
         run = run * low_ref[j * 8 : j * 8 + 8, :]
-    run = unpack(ret_ref[8:16, :])
+    run = unpack(seam_ref[1])
     for j in reversed(range(ROWS)):
         run = fe_ref[j * 8 : j * 8 + 8, :] + low_ref[j * 8 : j * 8 + 8, :] * run
         fe_ref[j * 8 : j * 8 + 8, :] = run * sp_ref[j * 8 : j * 8 + 8, :]
@@ -251,24 +257,27 @@
     w = w_ref[...]
 
     def carry(f, shift):
-        parts = [[ret_ref[pl.ds((16 * h + 8 * q) * 16 + f + shift, 8, stride=16), :] for h in range(2)] for q in range(2)]
+        parts = [[ret_ref[pl.ds((16 * h + 8 * q) * 12 + f + shift, 8, stride=12), :] for h in range(2)] for q in range(2)]
         return jnp.concatenate([jnp.concatenate(p, 1) for p in parts], 0)
 
     def planes(ref, j, f):
         v = ref[pl.ds(j * 8 + f, 8, stride=0), :]
         return jnp.where(mine, jnp.concatenate([v, v], 0), 0.0).astype(BF16)
 
-    def rise(t, run):
+    def rise(i, run):
         run = list(run)
-        for s in range(8):
+        t = i // 4
+        for u in range(2):
+            s = (i % 4) * 2 + u
+            j = i * 2 + u
             for f in range(FIELDS):
                 now = load_row(c_ref, f, t, s) + run[f]
-                sc_ref[f, pl.ds(pl.multiple_of(t * 128, 128) + s * 16, 16), :] = now * full(inv_ref, t * 8 + s, f)
-                run[f] = now * full(low_ref, t * 8 + s, f)
+                sc_ref[f, pl.ds(pl.multiple_of(i * 32, 32) + u * 16, 16), :] = now * full(inv_ref, j, f)
+                run[f] = now * full(low_ref, j, f)
         return tuple(run)
 
-    lax.fori_loop(0, 4, rise, tuple(carry(f, 0) for f in range(FIELDS)))
-    run = [carry(f, 8) for f in range(FIELDS)]
+    lax.fori_loop(0, 16, rise, tuple(carry(f, 0) for f in range(FIELDS)))
+    run = [carry(f, 5) for f in range(FIELDS)]
     copies = []
     for t in reversed(range(4)):
         for j in reversed(range(8 * t, 8 * t + 8)):
@@ -311,7 +320,7 @@
         in_specs=[pl.BlockSpec(memory_space=pltpu.HBM)] * 4,
         out_specs=[VM] * 6,
         scratch_shapes=[
-            pltpu.VMEM((3 * CELLS, 128), BF16),
+            pltpu.VMEM((384, 128), BF16),
             pltpu.VMEM((FIELDS, ROWS), F32),
             pltpu.VMEM((FIELDS, ROWS), F32),
             pltpu.SemaphoreType.DMA((8 * FIELDS + 3,)),
@@ -323,15 +332,15 @@
     count = lax.axis_size("stream")
     from_left = lax.ppermute(right, "stream", [(i, (i + 1) % count) for i in range(count)])
     from_right = lax.ppermute(left, "stream", [((i + 1) % count, i) for i in range(count)])
-    main = pl.pallas_call(
+    main, low, inv, sp = pl.pallas_call(
         sums_kernel,
-        out_shape=sds((WALLS * 16, 128), F32),
-        in_specs=[VM] * 3,
-        out_specs=VM,
+        out_shape=[sds((WALLS * 16, 128), F32), rows, rows, rows],
+        in_specs=[VM] * 6,
+        out_specs=[VM] * 4,
         compiler_params=params(),
         cost_estimate=pl.CostEstimate(flops=4000000, bytes_accessed=2600000, transcendentals=0),
         name="sums",
-    )(cells, rise, fall)
+    )(cells, rise, fall, lower, pivot, speed)
     send, ext = pl.pallas_call(
         merge_kernel,
         out_shape=[sds((WALLS, 16, 128), F32), rows],
@@ -341,22 +350,22 @@
         name="merge",
     )(main, rise, fall, unit, from_left, from_right)
     got = lax.all_to_all(send, "wall", 0, 0, tiled=True)
-    carries = pl.pallas_call(
+    carries, seam = pl.pallas_call(
         carry_kernel,
-        out_shape=sds((WALLS, 16, 128), F32),
+        out_shape=[sds((WALLS * 12, 128), F32), sds((2, 8, 128), F32)],
         in_specs=[VM],
-        out_specs=VM,
+        out_specs=[VM] * 2,
         scratch_shapes=[pltpu.VMEM((WALLS, 8, 128), F32)] * 2,
         compiler_params=params(),
         name="carry",
     )(got)
-    back = lax.all_to_all(carries, "wall", 0, 0, tiled=True)
+    back = lax.all_to_all(carries.reshape(WALLS, 3, 4, 128), "wall", 0, 0, tiled=True)
     out = pl.pallas_call(
         final_kernel,
         out_shape=sds((FIELDS * PLANES, 4, 2, 8, 128), F32),
-        in_specs=[VM] * 7,
+        in_specs=[VM] * 8,
         out_specs=pl.BlockSpec(memory_space=pl.ANY),
-        scratch_shapes=[pltpu.VMEM((ROWS * 8, 128), F32)] * 5
+        scratch_shapes=[pltpu.VMEM((ROWS * 8, 128), F32)] * 2
         + [
             pltpu.VMEM((FIELDS, ROWS * PLANES, CELLS), F32),
             pltpu.VMEM((2, FIELDS * PLANES * 8, 1024), BF16),
@@ -365,7 +374,7 @@
         ],
         compiler_params=params(),
         name="final",
-    )(cells, back.reshape(WALLS * 16, 128), lower, pivot, speed, ext, jnp.asarray(stencil))
+    )(cells, back.reshape(WALLS * 12, 128), seam, low, inv, sp, ext, jnp.asarray(stencil))
     return out.reshape(FIELDS, PLANES, 4, 2, 8, 128).transpose(0, 1, 2, 4, 3, 5).reshape(FIELDS, PLANES, ROWS, CELLS)
 
 

time: 53.8 us -> 52.2 us (0.970)
  Pallas kernels: 9.65 us -> 8.5 us
  blocking collectives: 29.7 us -> 29.1 us
    pallas_call x1, Pallas kernels: 4.54 us -> 3.46 us  [local(): pl.pallas_call(edge_kernel, out_shape=[sds((FIELDS, 8, 128), F32)] * 2 +...]
    all_to_all x1, blocking collectives: 12.4 us -> 11.8 us  [local(): lax.all_to_all(carries.reshape(WALLS, 3, 4, 128), 'wall', 0, 0, tiled=True)]
where the time goes in v4:
time: 52.2 us; the launch traced here: 51.9 us
  blocking collectives  29.1 us (56%)
  starting transfers between devices  14 us (27%)
  Pallas kernels  8.5 us (16%)
    all_to_all x1, blocking collectives, local(): got = lax.all_to_all(send, 'wall', 0, 0, tiled=True)  17.3 us
    all_to_all x1, blocking collectives, local(): lax.all_to_all(carries.reshape(WALLS, 3, 4, 128), 'wall', 0, 0, tiled=True)  11.8 us
    ppermute x1, starting transfers between devices, local(): lax.ppermute(left, 'stream', [((i + 1) % count, i) for i in range(count)])  9.5 us
    ppermute x1, starting transfers between devices, local(): lax.ppermute(right, 'stream', [(i, (i + 1) % count) for i in range(count)])  4.49 us
    pallas_call x1, Pallas kernels, local(): pl.pallas_call(final_kernel, out_shape=sds((FIELDS * PLANES, 4, 2, 8, 128...  4.02 us
    pallas_call x1, Pallas kernels, local(): pl.pallas_call(edge_kernel, out_shape=[sds((FIELDS, 8, 128), F32)] * 2 +...  3.46 us
  transfers between devices with their start and end apart: 2, of which 1 were waited for; matrix products, arithmetic and copies ran while one was open for 0% of the time, Pallas kernels for 1%

profile of v4, /device:TPU:1, one launch (start us, length us, event | category | flops | bytes accessed | tf_op | source)
XLA Modules:
  0.0 51.9 jit_solution(14923981980278547089)
XLA Ops:
  0.0 0.0 copy-start.2
  0.0 0.0 copy-start.1
  0.0 0.0 copy-start.3
  0.0 3.5 %edge.1 = (f32[5,8,128]{2,1,0:T(8,128)S(1)}, f32[5,8,128]{2,1,0:T(8,128)S(1)}, f32[5,4,2,16,8,128]{5,4,3,2,1,0:T(8,128)S(1)}, f32[256,128]{1,0:T(8,128)S(1)}, f3...) custom-call(f32[5,16,4,2,8,128]{5,4,3,2,1,0:T(8,128)} %bitcast.15, bf16[384,128]{1,0:T(8,128)(2,1)} %constant.4.clone.w_hbm, ...), custom_call_target="tpu_custom_call" | custom-call | tf_op jit(solution)/shard_map/edge/pallas_call | solution.py:317
  3.5 0.0 copy-start
  3.5 4.5 %collective-permute-start = (f32[5,8,128]{2,1,0:T(8,128)S(1)}, f32[5,8,128]{2,1,0:T(8,128)S(1)}, u32[]{:S(2)}, u32[]{:S(2)}) collective-permute-start(f32[5,8,128]{2,1,0:T(8,128)S(1)} %get-tuple-element.24), channel_id=1, source_target_pairs={{0,1},{1,2},{2,3},{3,4},{4,5},{5,6},{6,7},{7,8},{8,9},{9,10},{10,1... | collective-permute-start | bytes 61448 | tf_op jit(solution)/shard_map/ppermute | solution.py:333
  8.0 9.5 %collective-permute-start.1 = (f32[5,8,128]{2,1,0:T(8,128)S(1)}, f32[5,8,128]{2,1,0:T(8,128)S(1)}, u32[]{:S(2)}, u32[]{:S(2)}) collective-permute-start(f32[5,8,128]{2,1,0:T(8,128)S(1)} %get-tuple-element.25), channel_id=1, source_target_pairs={{1,0},{2,1},{3,2},{4,3},{5,4},{6,5},{7,6},{8,7},{9,8},{10,9},{11,1... | collective-permute-start | bytes 61448 | tf_op jit(solution)/shard_map/ppermute | solution.py:334
  17.5 0.0 copy-done.2
  17.5 0.0 copy-done.1
  17.5 0.0 copy-done.3
  17.5 0.6 %sums.1 = (f32[512,128]{1,0:T(8,128)S(1)}, f32[256,128]{1,0:T(8,128)S(1)}, f32[256,128]{1,0:T(8,128)S(1)}, f32[256,128]{1,0:T(8,128)S(1)}) custom-call(f32[5,1024,128]{2,1,0:T(8,128)S(1)} %bitcast.11, f32[256,128]{1,0:T(8,128)S(1)} %get-tuple-element.20.rise_ref, f32[256,128]{1,0:T(8,128)S(1)} %get-tuple-element.21.fall_ref, f32[5,32]{1,0:T(8,128)S(1)} %copy-done.1, ...), custom_call_target="tpu_custom_call" | custom-call | flops 4000000 | bytes 2600000 | tf_op jit(solution)/shard_map/sums/pallas_call | solution.py:335
  18.1 0.0 collective-permute-done.left_ref
  18.1 0.2 collective-permute-done.1.right_ref
  18.4 0.2 merge.1
  18.6 17.3 %all_to_all.10.in_ref = f32[32,16,128]{2,1,0:T(8,128)S(1)} all-to-all(f32[32,16,128]{2,1,0:T(8,128)S(1)} %get-tuple-element.26), channel_id=1, replica_groups=mesh['wall'=32,'stream'=16] {'wall'}, dimensions={0} | all-to-all | bytes 524288 | tf_op jit(solution)/shard_map/all_to_all | solution.py:352
  35.9 0.2 carry.1
  36.1 11.8 %all_to_all.11 = f32[32,3,4,128]{3,2,1,0:T(4,128)S(1)} all-to-all(f32[32,3,4,128]{3,2,1,0:T(4,128)S(1)} %bitcast.14), channel_id=1, replica_groups=mesh['wall'=32,'stream'=16] {'wall'}, dimensions={0} | all-to-all | bytes 393216 | tf_op jit(solution)/shard_map/all_to_all | solution.py:362
  47.9 0.0 copy-done
  47.9 4.0 %final.1 = f32[80,4,2,8,128]{4,3,2,1,0:T(8,128)} custom-call(f32[5,1024,128]{2,1,0:T(8,128)S(1)} %bitcast.12, f32[384,128]{1,0:T(8,128)S(1)} %bitcast.13, f32[2,8,128]{2,1,0:T(8,128)S(1)} %get-tuple-element.28.seam_ref, f32[256,128]{1,0:T(8,128)S(1)} %get-tuple-element.29.low_ref, f32[256,128]{1,0:T(8,128)S(1)} %get-tuple-element.30.inv_ref, ...), custom_call_target="tpu_custom_call" | custom-call | tf_op jit(solution)/shard_map/final/pallas_call | solution.py:363
Async XLA Ops:
  0.0 17.5 %copy-start.2 = (f32[5,32]{1,0:T(8,128)S(1)}, f32[5,32]{1,0:T(8,128)}, u32[]{:S(2)}) copy-start(f32[5,32]{1,0:T(8,128)} %pivot_ref.1) | copy-start | bytes 1924
  0.0 17.5 %copy-start.1 = (f32[5,32]{1,0:T(8,128)S(1)}, f32[5,32]{1,0:T(8,128)}, u32[]{:S(2)}) copy-start(f32[5,32]{1,0:T(8,128)} %lower_ref.1) | copy-start | bytes 1924
  0.0 17.5 %copy-start.3 = (f32[5,32]{1,0:T(8,128)S(1)}, f32[5,32]{1,0:T(8,128)}, u32[]{:S(2)}) copy-start(f32[5,32]{1,0:T(8,128)} %speed_ref.1) | copy-start | bytes 1924
  3.5 44.4 %copy-start = (bf16[1024,256]{1,0:T(8,128)(2,1)S(1)}, bf16[1024,256]{1,0:T(8,128)(2,1)}, u32[]{:S(2)}) copy-start(bf16[1024,256]{1,0:T(8,128)(2,1)} %constant.5.clone.w_ref) | copy-start | bytes 1572868
  3.5 14.7 %collective-permute-start = (f32[5,8,128]{2,1,0:T(8,128)S(1)}, f32[5,8,128]{2,1,0:T(8,128)S(1)}, u32[]{:S(2)}, u32[]{:S(2)}) collective-permute-start(f32[5,8,128]{2,1,0:T(8,128)S(1)} %get-tuple-element.24), channel_id=1, source_target_pairs={{0,1},{1,2},{2,3},{3,4},{4,5},{5,6},{6,7},{7,8},{8,9},{9,10},{10,1... | collective-permute-start | bytes 61448 | tf_op jit(solution)/shard_map/ppermute | solution.py:333
  8.0 10.4 %collective-permute-start.1 = (f32[5,8,128]{2,1,0:T(8,128)S(1)}, f32[5,8,128]{2,1,0:T(8,128)S(1)}, u32[]{:S(2)}, u32[]{:S(2)}) collective-permute-start(f32[5,8,128]{2,1,0:T(8,128)S(1)} %get-tuple-element.25), channel_id=1, source_target_pairs={{1,0},{2,1},{3,2},{4,3},{5,4},{6,5},{7,6},{8,7},{9,8},{10,9},{11,1... | collective-permute-start | bytes 61448 | tf_op jit(solution)/shard_map/ppermute | solution.py:334

commit v5 on v4

--- a/solution.py
+++ b/solution.py
@@ -64,24 +64,20 @@
     return lax.broadcasted_iota(jnp.int32, shape, len(shape) - 2)
 
 
-def edge_kernel(c_hbm, w_hbm, lower_hbm, pivot_hbm, left_ref, right_ref, c_ref, rise_ref, fall_ref, unit_ref, w_ref, lower_ref, pivot_ref, sem):
+def edge_kernel(c_hbm, w_hbm, lower_hbm, pivot_hbm, left_ref, right_ref, c_ref, rise_ref, fall_ref, gain_ref, unit_ref, w_ref, lower_ref, pivot_ref, sem):
     small = [
         pltpu.make_async_copy(a, b, sem.at[i])
         for i, (a, b) in enumerate([(lower_hbm, lower_ref), (pivot_hbm, pivot_ref), (w_hbm, w_ref)])
     ]
     big = [
-        [
-            pltpu.make_async_copy(c_hbm.at[f, :, t, h], c_ref.at[f, t, h], sem.at[3 + (f * 4 + t) * 2 + h])
-            for t in range(4)
-            for h in range(2)
-        ]
+        [pltpu.make_async_copy(c_hbm.at[f, p], c_ref.at[f, :, :, p], sem.at[3 + f * PLANES + p]) for p in range(PLANES)]
         for f in range(FIELDS)
     ]
     for copy in small + sum(big, []):
         copy.start()
     small[0].wait()
     small[1].wait()
-    weights(lower_ref, pivot_ref, rise_ref, fall_ref, unit_ref)
+    weights(lower_ref, pivot_ref, rise_ref, fall_ref, gain_ref, unit_ref)
     small[2].wait()
     w = w_ref[...]
     plane, lane = lanes((8, 128)) % 16, lanes((8, 128)) // 32
@@ -121,13 +117,14 @@
         out_ref[j * 8 : j * 8 + FIELDS, :] = jnp.broadcast_to(value[:, j : j + 1], (FIELDS, 128))
 
 
-def weights(lower_ref, pivot_ref, rise_ref, fall_ref, unit_ref):
+def weights(lower_ref, pivot_ref, rise_ref, fall_ref, gain_ref, unit_ref):
     low, piv = lower_ref[...], 1.0 / pivot_ref[...]
     wide = lambda v, j: jnp.broadcast_to(v[:, j : j + 1], (FIELDS, 128))
     entry = jnp.ones((FIELDS, 128), F32)
     direct, spread = [], jnp.zeros((FIELDS, 128), F32)
     for j in range(ROWS):
         direct.append(entry * wide(piv, j))
+        gain_ref[j * 8 : j * 8 + FIELDS, :] = direct[j]
         spread = spread + entry * direct[j]
         entry = entry * wide(low, j)
     leave, first = None, None
@@ -141,21 +138,23 @@
     unit_ref[1, :FIELDS, :] = spread
 
 
-def sums_kernel(c_ref, rise_ref, fall_ref, lower_ref, pivot_ref, speed_ref, out_ref, low_ref, inv_ref, sp_ref):
+def sums_kernel(c_ref, fall_ref, lower_ref, pivot_ref, speed_ref, out_ref, base_ref, low_ref, inv_ref, sp_ref):
     spread_rows(lower_ref[...], low_ref)
     spread_rows(1.0 / pivot_ref[...], inv_ref)
     spread_rows(speed_ref[...], sp_ref)
     for f in range(FIELDS):
-        up = jnp.zeros((PLANES, CELLS), F32)
+        run = jnp.zeros((PLANES, CELLS), F32)
         down = jnp.zeros((PLANES, CELLS), F32)
         for j in range(ROWS):
             v = load_row(c_ref, f, j // 8, j % 8)
-            up = up + full(rise_ref, j, f) * v
             down = down + full(fall_ref, j, f) * v
+            run = v + run
+            base_ref[f, j * 16 : j * 16 + 16, :] = run * full(inv_ref, j, f)
+            run = run * full(low_ref, j, f)
         for h in range(2):
             for q in range(2):
                 base = (16 * h + 8 * q) * 16 + f
-                out_ref[pl.ds(base, 8, stride=16), :] = up[8 * q : 8 * q + 8, 128 * h : 128 * h + 128]
+                out_ref[pl.ds(base, 8, stride=16), :] = run[8 * q : 8 * q + 8, 128 * h : 128 * h + 128]
                 out_ref[pl.ds(base + 8, 8, stride=16), :] = down[8 * q : 8 * q + 8, 128 * h : 128 * h + 128]
 
 
@@ -225,7 +224,7 @@
 
 
 def final_kernel(
-    c_ref, ret_ref, seam_ref, low_ref, inv_ref, sp_ref, ext_ref, w_ref, o_ref, fe_ref, fl_ref, sc_ref, lhs_ref, res_ref, sem
+    base_ref, ret_ref, seam_ref, low_ref, inv_ref, gain_ref, sp_ref, ext_ref, w_ref, o_ref, fe_ref, fl_ref, in_ref, sc_ref, lhs_ref, res_ref, sem
 ):
     sub, lane = sublanes((8, 128)), lanes((8, 128))
 
@@ -264,30 +263,20 @@
         v = ref[pl.ds(j * 8 + f, 8, stride=0), :]
         return jnp.where(mine, jnp.concatenate([v, v], 0), 0.0).astype(BF16)
 
-    def rise(i, run):
-        run = list(run)
-        t = i // 4
-        for u in range(2):
-            s = (i % 4) * 2 + u
-            j = i * 2 + u
-            for f in range(FIELDS):
-                now = load_row(c_ref, f, t, s) + run[f]
-                sc_ref[f, pl.ds(pl.multiple_of(i * 32, 32) + u * 16, 16), :] = now * full(inv_ref, j, f)
-                run[f] = now * full(low_ref, j, f)
-        return tuple(run)
-
-    lax.fori_loop(0, 16, rise, tuple(carry(f, 0) for f in range(FIELDS)))
+    for f in range(FIELDS):
+        in_ref[f] = carry(f, 0)
     run = [carry(f, 5) for f in range(FIELDS)]
     copies = []
     for t in reversed(range(4)):
         for j in reversed(range(8 * t, 8 * t + 8)):
             for f in range(FIELDS):
-                run[f] = sc_ref[f, j * 16 : j * 16 + 16, :] + full(low_ref, j, f) * run[f]
+                scaled = base_ref[f, j * 16 : j * 16 + 16, :] + full(gain_ref, j, f) * in_ref[f]
+                run[f] = scaled + full(low_ref, j, f) * run[f]
                 sc_ref[f, j * 16 : j * 16 + 16, :] = run[f]
                 hi, lo = halves(run[f] * full(sp_ref, j, f))
                 at = f * 128 + (j % 8) * 16
-                lhs_ref[t % 2, at : at + 16, :] = jnp.concatenate([hi, lo, hi, planes(fe_ref, j, f), planes(fl_ref, j, f)], 1)
-        out = jnp.dot(lhs_ref[t % 2], w, preferred_element_type=F32)
+                lhs_ref[t, at : at + 16, :] = jnp.concatenate([hi, lo, hi, planes(fe_ref, j, f), planes(fl_ref, j, f)], 1)
+        out = jnp.dot(lhs_ref[t], w, preferred_element_type=F32)
         for f in range(FIELDS):
             for s in range(8):
                 j, at = 8 * t + s, f * 128 + s * 16
@@ -313,17 +302,17 @@
     stencil, edge = tables()
     sds = jax.ShapeDtypeStruct
     flat = cotangent.reshape(FIELDS, PLANES, 4, 8, 2, 128).transpose(0, 1, 2, 4, 3, 5)
-    rows = sds((ROWS * 8, 128), F32)
-    left, right, cells, rise, fall, unit = pl.pallas_call(
+    rows = sds((ROWS * 8 + 8, 128), F32)
+    left, right, cells, rise, fall, gain, unit = pl.pallas_call(
         edge_kernel,
-        out_shape=[sds((FIELDS, 8, 128), F32)] * 2 + [sds((FIELDS, 4, 2, PLANES, 8, 128), F32), rows, rows, sds((2, 8, 128), F32)],
+        out_shape=[sds((FIELDS, 8, 128), F32)] * 2 + [sds((FIELDS, 4, 2, PLANES, 8, 128), F32), rows, rows, rows, sds((2, 8, 128), F32)],
         in_specs=[pl.BlockSpec(memory_space=pltpu.HBM)] * 4,
-        out_specs=[VM] * 6,
+        out_specs=[VM] * 7,
         scratch_shapes=[
             pltpu.VMEM((384, 128), BF16),
             pltpu.VMEM((FIELDS, ROWS), F32),
             pltpu.VMEM((FIELDS, ROWS), F32),
-            pltpu.SemaphoreType.DMA((8 * FIELDS + 3,)),
+            pltpu.SemaphoreType.DMA((PLANES * FIELDS + 3,)),
         ],
         compiler_params=params(),
         name="edge",
@@ -332,15 +321,15 @@
     count = lax.axis_size("stream")
     from_left = lax.ppermute(right, "stream", [(i, (i + 1) % count) for i in range(count)])
     from_right = lax.ppermute(left, "stream", [((i + 1) % count, i) for i in range(count)])
-    main, low, inv, sp = pl.pallas_call(
+    main, base, low, inv, sp = pl.pallas_call(
         sums_kernel,
-        out_shape=[sds((WALLS * 16, 128), F32), rows, rows, rows],
-        in_specs=[VM] * 6,
-        out_specs=[VM] * 4,
+        out_shape=[sds((WALLS * 16, 128), F32), sds((FIELDS, ROWS * PLANES, CELLS), F32), rows, rows, rows],
+        in_specs=[VM] * 5,
+        out_specs=[VM] * 5,
         compiler_params=params(),
         cost_estimate=pl.CostEstimate(flops=4000000, bytes_accessed=2600000, transcendentals=0),
         name="sums",
-    )(cells, rise, fall, lower, pivot, speed)
+    )(cells, fall, lower, pivot, speed)
     send, ext = pl.pallas_call(
         merge_kernel,
         out_shape=[sds((WALLS, 16, 128), F32), rows],
@@ -363,18 +352,19 @@
     out = pl.pallas_call(
         final_kernel,
         out_shape=sds((FIELDS * PLANES, 4, 2, 8, 128), F32),
-        in_specs=[VM] * 8,
+        in_specs=[VM] * 9,
         out_specs=pl.BlockSpec(memory_space=pl.ANY),
-        scratch_shapes=[pltpu.VMEM((ROWS * 8, 128), F32)] * 2
+        scratch_shapes=[pltpu.VMEM((ROWS * 8 + 8, 128), F32)] * 2
         + [
+            pltpu.VMEM((FIELDS, PLANES, CELLS), F32),
             pltpu.VMEM((FIELDS, ROWS * PLANES, CELLS), F32),
-            pltpu.VMEM((2, FIELDS * PLANES * 8, 1024), BF16),
+            pltpu.VMEM((4, FIELDS * PLANES * 8, 1024), BF16),
             pltpu.VMEM((4, 2, FIELDS * PLANES * 8, 128), F32),
             pltpu.SemaphoreType.DMA((8,)),
         ],
         compiler_params=params(),
         name="final",
-    )(cells, back.reshape(WALLS * 12, 128), seam, low, inv, sp, ext, jnp.asarray(stencil))
+    )(base, back.reshape(WALLS * 12, 128), seam, low, inv, gain, sp, ext, jnp.asarray(stencil))
     return out.reshape(FIELDS, PLANES, 4, 2, 8, 128).transpose(0, 1, 2, 4, 3, 5).reshape(FIELDS, PLANES, ROWS, CELLS)
 
 

time: 52.2 us -> 51.8 us (level)
    pallas_call x1, Pallas kernels: 4.02 us -> 3.32 us  [local(): pl.pallas_call(final_kernel, out_shape=sds((FIELDS * PLANES, 4, 2, 8, 128...]
  transfers between devices with their start and end apart: 2 -> 2, of which waited for: 1 -> 0; matrix products, arithmetic and copies ran while one was open for 0% -> 0% of each run, Pallas kernels for 1% -> 2%
where the time goes in v5:
time: 51.8 us; the launch traced here: 51.5 us
  blocking collectives  29 us (56%)
  starting transfers between devices  14 us (27%)
  Pallas kernels  8.38 us (16%)
    all_to_all x1, blocking collectives, local(): got = lax.all_to_all(send, 'wall', 0, 0, tiled=True)  17.2 us
    all_to_all x1, blocking collectives, local(): lax.all_to_all(carries.reshape(WALLS, 3, 4, 128), 'wall', 0, 0, tiled=True)  11.8 us
    ppermute x1, starting transfers between devices, local(): lax.ppermute(left, 'stream', [((i + 1) % count, i) for i in range(count)])  9.5 us
    ppermute x1, starting transfers between devices, local(): lax.ppermute(right, 'stream', [(i, (i + 1) % count) for i in range(count)])  4.49 us
    pallas_call x1, Pallas kernels, local(): pl.pallas_call(edge_kernel, out_shape=[sds((FIELDS, 8, 128), F32)] * 2 +...  3.78 us
    pallas_call x1, Pallas kernels, local(): pl.pallas_call(final_kernel, out_shape=sds((FIELDS * PLANES, 4, 2, 8, 128...  3.32 us
  transfers between devices with their start and end apart: 2, of which 0 were waited for; matrix products, arithmetic and copies ran while one was open for 0% of the time, Pallas kernels for 2%

profile of v5, /device:TPU:1, one launch (start us, length us, event | category | flops | bytes accessed | tf_op | source)
XLA Modules:
  0.0 51.5 jit_solution(17058821825517507001)
XLA Ops:
  0.0 0.0 copy-start.2
  0.0 0.0 copy-start.1
  0.0 0.0 copy-start.3
  0.0 3.8 %edge.1 = (f32[5,8,128]{2,1,0:T(8,128)S(1)}, f32[5,8,128]{2,1,0:T(8,128)S(1)}, f32[5,4,2,16,8,128]{5,4,3,2,1,0:T(8,128)S(1)}, f32[264,128]{1,0:T(8,128)S(1)}, f3...) custom-call(f32[5,16,4,2,8,128]{5,4,3,2,1,0:T(8,128)} %bitcast.14, ...), custom_call_target="tpu_custom_call" | custom-call | tf_op jit(solution)/shard_map/edge/pallas_call | solution.py:306
  3.8 0.0 copy-start
  3.8 4.5 %collective-permute-start = (f32[5,8,128]{2,1,0:T(8,128)S(1)}, f32[5,8,128]{2,1,0:T(8,128)S(1)}, u32[]{:S(2)}, u32[]{:S(2)}) collective-permute-start(f32[5,8,128]{2,1,0:T(8,128)S(1)} %get-tuple-element.27), channel_id=1, source_target_pairs={{0,1},{1,2},{2,3},{3,4},{4,5},{5,6},{6,7},{7,8},{8,9},{9,10},{10,1... | collective-permute-start | bytes 61448 | tf_op jit(solution)/shard_map/ppermute | solution.py:322
  8.3 9.5 %collective-permute-start.1 = (f32[5,8,128]{2,1,0:T(8,128)S(1)}, f32[5,8,128]{2,1,0:T(8,128)S(1)}, u32[]{:S(2)}, u32[]{:S(2)}) collective-permute-start(f32[5,8,128]{2,1,0:T(8,128)S(1)} %get-tuple-element.28), channel_id=1, source_target_pairs={{1,0},{2,1},{3,2},{4,3},{5,4},{6,5},{7,6},{8,7},{9,8},{10,9},{11,1... | collective-permute-start | bytes 61448 | tf_op jit(solution)/shard_map/ppermute | solution.py:323
  17.8 0.0 copy-done.2
  17.8 0.0 copy-done.1
  17.8 0.0 copy-done.3
  17.8 0.9 %sums.1 = (f32[512,128]{1,0:T(8,128)S(1)}, f32[5,512,256]{2,1,0:T(8,128)S(1)}, f32[264,128]{1,0:T(8,128)S(1)}, f32[264,128]{1,0:T(8,128)S(1)}, f32[264,128]{1,0:T(8,128)S(1)}) custom-call(f32[5,1024,128]{2,1,0:T(8,128)S(1)} %bitcast.11, f32[264,128]{1,0:T(8,128)S(1)} %get-tuple-element.22.fall_ref, f32[5,32]{1,0:T(8,128)S(1)} %copy-done.1, ...), custom_call_target="tpu_custom_call" | custom-call | flops 4000000 | bytes 2600000 | tf_op jit(solution)/shard_map/sums/pallas_call | solution.py:324
  18.7 0.0 collective-permute-done.left_ref
  18.7 0.0 collective-permute-done.1.right_ref
  18.7 0.2 merge.1
  19.0 17.2 %all_to_all.10.in_ref = f32[32,16,128]{2,1,0:T(8,128)S(1)} all-to-all(f32[32,16,128]{2,1,0:T(8,128)S(1)} %get-tuple-element.29), channel_id=1, replica_groups=mesh['wall'=32,'stream'=16] {'wall'}, dimensions={0} | all-to-all | bytes 524288 | tf_op jit(solution)/shard_map/all_to_all | solution.py:341
  36.2 0.2 carry.1
  36.4 11.8 %all_to_all.11 = f32[32,3,4,128]{3,2,1,0:T(4,128)S(1)} all-to-all(f32[32,3,4,128]{3,2,1,0:T(4,128)S(1)} %bitcast.13), channel_id=1, replica_groups=mesh['wall'=32,'stream'=16] {'wall'}, dimensions={0} | all-to-all | bytes 393216 | tf_op jit(solution)/shard_map/all_to_all | solution.py:351
  48.2 0.0 copy-done
  48.2 3.3 %final.1 = f32[80,4,2,8,128]{4,3,2,1,0:T(8,128)} custom-call(f32[5,512,256]{2,1,0:T(8,128)S(1)} %get-tuple-element.23.base_ref, f32[384,128]{1,0:T(8,128)S(1)} %bitcast.12, f32[2,8,128]{2,1,0:T(8,128)S(1)} %get-tuple-element.31.seam_ref, f32[264,128]{1,0:T(8,128)S(1)} %get-tuple-element.32.low_ref, f32[264,128]{1,0:T(8,128)S(1)} %get-tuple-element.33.inv_ref, ...), custom_call_target="tpu_custom_call" | custom-call | tf_op jit(solution)/shard_map/final/pallas_call | solution.py:352
Async XLA Ops:
  0.0 17.8 %copy-start.2 = (f32[5,32]{1,0:T(8,128)S(1)}, f32[5,32]{1,0:T(8,128)}, u32[]{:S(2)}) copy-start(f32[5,32]{1,0:T(8,128)} %pivot_ref.1) | copy-start | bytes 1924
  0.0 17.8 %copy-start.1 = (f32[5,32]{1,0:T(8,128)S(1)}, f32[5,32]{1,0:T(8,128)}, u32[]{:S(2)}) copy-start(f32[5,32]{1,0:T(8,128)} %lower_ref.1) | copy-start | bytes 1924
  0.0 17.8 %copy-start.3 = (f32[5,32]{1,0:T(8,128)S(1)}, f32[5,32]{1,0:T(8,128)}, u32[]{:S(2)}) copy-start(f32[5,32]{1,0:T(8,128)} %speed_ref.1) | copy-start | bytes 1924
  3.8 44.4 %copy-start = (bf16[1024,256]{1,0:T(8,128)(2,1)S(1)}, bf16[1024,256]{1,0:T(8,128)(2,1)}, u32[]{:S(2)}) copy-start(bf16[1024,256]{1,0:T(8,128)(2,1)} %constant.5.clone.w_ref) | copy-start | bytes 1572868
  3.8 14.9 %collective-permute-start = (f32[5,8,128]{2,1,0:T(8,128)S(1)}, f32[5,8,128]{2,1,0:T(8,128)S(1)}, u32[]{:S(2)}, u32[]{:S(2)}) collective-permute-start(f32[5,8,128]{2,1,0:T(8,128)S(1)} %get-tuple-element.27), channel_id=1, source_target_pairs={{0,1},{1,2},{2,3},{3,4},{4,5},{5,6},{6,7},{7,8},{8,9},{9,10},{10,1... | collective-permute-start | bytes 61448 | tf_op jit(solution)/shard_map/ppermute | solution.py:322
  8.3 10.4 %collective-permute-start.1 = (f32[5,8,128]{2,1,0:T(8,128)S(1)}, f32[5,8,128]{2,1,0:T(8,128)S(1)}, u32[]{:S(2)}, u32[]{:S(2)}) collective-permute-start(f32[5,8,128]{2,1,0:T(8,128)S(1)} %get-tuple-element.28), channel_id=1, source_target_pairs={{1,0},{2,1},{3,2},{4,3},{5,4},{6,5},{7,6},{8,7},{9,8},{10,9},{11,1... | collective-permute-start | bytes 61448 | tf_op jit(solution)/shard_map/ppermute | solution.py:323

commit v6 on v5

--- a/solution.py
+++ b/solution.py
@@ -70,20 +70,20 @@
         for i, (a, b) in enumerate([(lower_hbm, lower_ref), (pivot_hbm, pivot_ref), (w_hbm, w_ref)])
     ]
     big = [
-        [pltpu.make_async_copy(c_hbm.at[f, p], c_ref.at[f, :, :, p], sem.at[3 + f * PLANES + p]) for p in range(PLANES)]
+        [
+            pltpu.make_async_copy(c_hbm.at[f, :, t, h], c_ref.at[f, t, h], sem.at[3 + (f * 4 + t) * 2 + h])
+            for t in range(4)
+            for h in range(2)
+        ]
         for f in range(FIELDS)
     ]
-    for copy in small + sum(big, []):
+    for copy in [small[2]] + big[0] + big[1] + small[:2] + sum(big[2:], []):
         copy.start()
-    small[0].wait()
-    small[1].wait()
-    weights(lower_ref, pivot_ref, rise_ref, fall_ref, gain_ref, unit_ref)
     small[2].wait()
     w = w_ref[...]
     plane, lane = lanes((8, 128)) % 16, lanes((8, 128)) // 32
-    for f in range(FIELDS):
-        for copy in big[f]:
-            copy.wait()
+
+    def edges(f):
         ends = [c_ref[f, :, h].reshape(PLANES * ROWS, 128) for h in range(2)]
         hi, lo = halves(jnp.where(lanes((PLANES * ROWS, 128)) < 64, ends[0], ends[1]))
         sums = jnp.dot(jnp.concatenate([hi, lo, hi], axis=1), w, preferred_element_type=F32)
@@ -101,6 +101,16 @@
             right = jnp.where(lane == q, pltpu.roll(part, (32 * q + 96) % 128, 1) if q != 1 else part, right)
         left_ref[f] = left
         right_ref[f] = right
+
+    for copy in big[0] + big[1]:
+        copy.wait()
+    edges(0)
+    edges(1)
+    for copy in small[:2] + sum(big[2:], []):
+        copy.wait()
+    weights(lower_ref, pivot_ref, rise_ref, fall_ref, gain_ref, unit_ref)
+    for f in range(2, FIELDS):
+        edges(f)
 
 
 def load_row(ref, f, t, s):
@@ -312,7 +322,7 @@
             pltpu.VMEM((384, 128), BF16),
             pltpu.VMEM((FIELDS, ROWS), F32),
             pltpu.VMEM((FIELDS, ROWS), F32),
-            pltpu.SemaphoreType.DMA((PLANES * FIELDS + 3,)),
+            pltpu.SemaphoreType.DMA((8 * FIELDS + 3,)),
         ],
         compiler_params=params(),
         name="edge",

time: 51.8 us -> 50.9 us (0.983)
  Pallas kernels: 8.38 us -> 7.43 us
    pallas_call x1, Pallas kernels: 3.78 us -> 2.82 us  [local(): pl.pallas_call(edge_kernel, out_shape=[sds((FIELDS, 8, 128), F32)] * 2 +...]
where the time goes in v6:
time: 50.9 us; the launch traced here: 50.6 us
  blocking collectives  29.1 us (57%)
  starting transfers between devices  14 us (28%)
  Pallas kernels  7.43 us (15%)
    all_to_all x1, blocking collectives, local(): got = lax.all_to_all(send, 'wall', 0, 0, tiled=True)  17.3 us
    all_to_all x1, blocking collectives, local(): lax.all_to_all(carries.reshape(WALLS, 3, 4, 128), 'wall', 0, 0, tiled=True)  11.8 us
    ppermute x1, starting transfers between devices, local(): lax.ppermute(left, 'stream', [((i + 1) % count, i) for i in range(count)])  9.47 us
    ppermute x1, starting transfers between devices, local(): lax.ppermute(right, 'stream', [(i, (i + 1) % count) for i in range(count)])  4.49 us
    pallas_call x1, Pallas kernels, local(): pl.pallas_call(final_kernel, out_shape=sds((FIELDS * PLANES, 4, 2, 8, 128...  3.32 us
    pallas_call x1, Pallas kernels, local(): pl.pallas_call(edge_kernel, out_shape=[sds((FIELDS, 8, 128), F32)] * 2 +...  2.82 us
  transfers between devices with their start and end apart: 2, of which 0 were waited for; matrix products, arithmetic and copies ran while one was open for 0% of the time, Pallas kernels for 2%

profile of v6, /device:TPU:1, one launch (start us, length us, event | category | flops | bytes accessed | tf_op | source)
XLA Modules:
  0.0 50.6 jit_solution(16136436119273484526)
XLA Ops:
  0.0 0.0 copy-start.2
  0.0 0.0 copy-start.1
  0.0 0.0 copy-start.3
  0.0 2.8 %edge.1 = (f32[5,8,128]{2,1,0:T(8,128)S(1)}, f32[5,8,128]{2,1,0:T(8,128)S(1)}, f32[5,4,2,16,8,128]{5,4,3,2,1,0:T(8,128)S(1)}, f32[264,128]{1,0:T(8,128)S(1)}, f3...) custom-call(f32[5,16,4,2,8,128]{5,4,3,2,1,0:T(8,128)} %bitcast.14, ...), custom_call_target="tpu_custom_call" | custom-call | tf_op jit(solution)/shard_map/edge/pallas_call | solution.py:316
  2.8 0.0 copy-start
  2.9 4.5 %collective-permute-start = (f32[5,8,128]{2,1,0:T(8,128)S(1)}, f32[5,8,128]{2,1,0:T(8,128)S(1)}, u32[]{:S(2)}, u32[]{:S(2)}) collective-permute-start(f32[5,8,128]{2,1,0:T(8,128)S(1)} %get-tuple-element.27), channel_id=1, source_target_pairs={{0,1},{1,2},{2,3},{3,4},{4,5},{5,6},{6,7},{7,8},{8,9},{9,10},{10,1... | collective-permute-start | bytes 61448 | tf_op jit(solution)/shard_map/ppermute | solution.py:332
  7.3 9.5 %collective-permute-start.1 = (f32[5,8,128]{2,1,0:T(8,128)S(1)}, f32[5,8,128]{2,1,0:T(8,128)S(1)}, u32[]{:S(2)}, u32[]{:S(2)}) collective-permute-start(f32[5,8,128]{2,1,0:T(8,128)S(1)} %get-tuple-element.28), channel_id=1, source_target_pairs={{1,0},{2,1},{3,2},{4,3},{5,4},{6,5},{7,6},{8,7},{9,8},{10,9},{11,1... | collective-permute-start | bytes 61448 | tf_op jit(solution)/shard_map/ppermute | solution.py:333
  16.8 0.0 copy-done.2
  16.8 0.0 copy-done.1
  16.8 0.0 copy-done.3
  16.9 0.9 %sums.1 = (f32[512,128]{1,0:T(8,128)S(1)}, f32[5,512,256]{2,1,0:T(8,128)S(1)}, f32[264,128]{1,0:T(8,128)S(1)}, f32[264,128]{1,0:T(8,128)S(1)}, f32[264,128]{1,0:T(8,128)S(1)}) custom-call(f32[5,1024,128]{2,1,0:T(8,128)S(1)} %bitcast.11, f32[264,128]{1,0:T(8,128)S(1)} %get-tuple-element.22.fall_ref, f32[5,32]{1,0:T(8,128)S(1)} %copy-done.1, ...), custom_call_target="tpu_custom_call" | custom-call | flops 4000000 | bytes 2600000 | tf_op jit(solution)/shard_map/sums/pallas_call | solution.py:334
  17.7 0.0 collective-permute-done.left_ref
  17.7 0.0 collective-permute-done.1.right_ref
  17.8 0.2 merge.1
  18.0 17.3 %all_to_all.10.in_ref = f32[32,16,128]{2,1,0:T(8,128)S(1)} all-to-all(f32[32,16,128]{2,1,0:T(8,128)S(1)} %get-tuple-element.29), channel_id=1, replica_groups=mesh['wall'=32,'stream'=16] {'wall'}, dimensions={0} | all-to-all | bytes 524288 | tf_op jit(solution)/shard_map/all_to_all | solution.py:351
  35.2 0.2 carry.1
  35.5 11.8 %all_to_all.11 = f32[32,3,4,128]{3,2,1,0:T(4,128)S(1)} all-to-all(f32[32,3,4,128]{3,2,1,0:T(4,128)S(1)} %bitcast.13), channel_id=1, replica_groups=mesh['wall'=32,'stream'=16] {'wall'}, dimensions={0} | all-to-all | bytes 393216 | tf_op jit(solution)/shard_map/all_to_all | solution.py:361
  47.2 0.0 copy-done
  47.2 3.3 %final.1 = f32[80,4,2,8,128]{4,3,2,1,0:T(8,128)} custom-call(f32[5,512,256]{2,1,0:T(8,128)S(1)} %get-tuple-element.23.base_ref, f32[384,128]{1,0:T(8,128)S(1)} %bitcast.12, f32[2,8,128]{2,1,0:T(8,128)S(1)} %get-tuple-element.31.seam_ref, f32[264,128]{1,0:T(8,128)S(1)} %get-tuple-element.32.low_ref, f32[264,128]{1,0:T(8,128)S(1)} %get-tuple-element.33.inv_ref, ...), custom_call_target="tpu_custom_call" | custom-call | tf_op jit(solution)/shard_map/final/pallas_call | solution.py:362
Async XLA Ops:
  0.0 16.8 %copy-start.2 = (f32[5,32]{1,0:T(8,128)S(1)}, f32[5,32]{1,0:T(8,128)}, u32[]{:S(2)}) copy-start(f32[5,32]{1,0:T(8,128)} %pivot_ref.1) | copy-start | bytes 1924
  0.0 16.8 %copy-start.1 = (f32[5,32]{1,0:T(8,128)S(1)}, f32[5,32]{1,0:T(8,128)}, u32[]{:S(2)}) copy-start(f32[5,32]{1,0:T(8,128)} %lower_ref.1) | copy-start | bytes 1924
  0.0 16.8 %copy-start.3 = (f32[5,32]{1,0:T(8,128)S(1)}, f32[5,32]{1,0:T(8,128)}, u32[]{:S(2)}) copy-start(f32[5,32]{1,0:T(8,128)} %speed_ref.1) | copy-start | bytes 1924
  2.8 44.4 %copy-start = (bf16[1024,256]{1,0:T(8,128)(2,1)S(1)}, bf16[1024,256]{1,0:T(8,128)(2,1)}, u32[]{:S(2)}) copy-start(bf16[1024,256]{1,0:T(8,128)(2,1)} %constant.5.clone.w_ref) | copy-start | bytes 1572868
  2.9 14.9 %collective-permute-start = (f32[5,8,128]{2,1,0:T(8,128)S(1)}, f32[5,8,128]{2,1,0:T(8,128)S(1)}, u32[]{:S(2)}, u32[]{:S(2)}) collective-permute-start(f32[5,8,128]{2,1,0:T(8,128)S(1)} %get-tuple-element.27), channel_id=1, source_target_pairs={{0,1},{1,2},{2,3},{3,4},{4,5},{5,6},{6,7},{7,8},{8,9},{9,10},{10,1... | collective-permute-start | bytes 61448 | tf_op jit(solution)/shard_map/ppermute | solution.py:332
  7.3 10.4 %collective-permute-start.1 = (f32[5,8,128]{2,1,0:T(8,128)S(1)}, f32[5,8,128]{2,1,0:T(8,128)S(1)}, u32[]{:S(2)}, u32[]{:S(2)}) collective-permute-start(f32[5,8,128]{2,1,0:T(8,128)S(1)} %get-tuple-element.28), channel_id=1, source_target_pairs={{1,0},{2,1},{3,2},{4,3},{5,4},{6,5},{7,6},{8,7},{9,8},{10,9},{11,1... | collective-permute-start | bytes 61448 | tf_op jit(solution)/shard_map/ppermute | solution.py:333

commit v7 on v6

--- a/solution.py
+++ b/solution.py
@@ -163,9 +163,9 @@
             run = run * full(low_ref, j, f)
         for h in range(2):
             for q in range(2):
-                base = (16 * h + 8 * q) * 16 + f
-                out_ref[pl.ds(base, 8, stride=16), :] = run[8 * q : 8 * q + 8, 128 * h : 128 * h + 128]
-                out_ref[pl.ds(base + 8, 8, stride=16), :] = down[8 * q : 8 * q + 8, 128 * h : 128 * h + 128]
+                base = (16 * h + 8 * q) * 12 + f
+                out_ref[pl.ds(base, 8, stride=12), :] = run[8 * q : 8 * q + 8, 128 * h : 128 * h + 128]
+                out_ref[pl.ds(base + 5, 8, stride=12), :] = down[8 * q : 8 * q + 8, 128 * h : 128 * h + 128]
 
 
 def merge_kernel(main_ref, rise_ref, fall_ref, unit_ref, left_ref, right_ref, out_ref, ext_ref):
@@ -185,74 +185,70 @@
             down = down + fall_ref[pl.ds(64 * q + f, 8, stride=8), :] * v
         ups.append(jnp.sum(up, axis=0, keepdims=True))
         downs.append(jnp.sum(down, axis=0, keepdims=True))
-    row = sublanes((FIELDS, 128))
-    lane5 = lanes((FIELDS, 128))
-    coef = jnp.where(lane5 == 64 + row, unit_ref[0, :FIELDS, :], 0.0)
-    coef = jnp.where(lane5 == 72 + row, unit_ref[1, :FIELDS, :], coef)
-    coef = jnp.sum(coef, axis=0, keepdims=True)
-    lane1 = lanes((1, 128))
-    sub = sublanes((8, 128))
-
-    def pack(v, last):
-        rows = [jnp.where(lane1 < 64, v[0], v[1]), jnp.where(lane1 < 64, v[2], v[3]), jnp.where(lane1 < 64, v[4], last)]
-        return jnp.where(sub == 5, rows[0], jnp.where(sub == 6, rows[1], rows[2]))
-
-    tail_up, tail_down = pack(ups, coef), pack(downs, jnp.zeros((1, 128), F32))
-    for k in range(WALLS):
-        out_ref[k, :8, :] = jnp.where(sub < 5, main_ref[16 * k : 16 * k + 8, :], tail_up)
-        out_ref[k, 8:, :] = jnp.where(sub < 5, main_ref[16 * k + 8 : 16 * k + 16, :], tail_down)
-
-
-def carry_kernel(in_ref, out_ref, seam_ref, through_ref, crest_ref):
-    me = lax.axis_index("wall")
+    row, lane5, lane1 = sublanes((FIELDS, 128)), lanes((FIELDS, 128)), lanes((1, 128))
+    out_ref[...] = main_ref[...]
+    for i, v in enumerate([ups, downs]):
+        gains = jnp.sum(jnp.where(lane5 == 96 + row, unit_ref[i, :FIELDS, :], 0.0), axis=0, keepdims=True)
+        for e in range(4):
+            tail = gains
+            for f in range(FIELDS):
+                shift = (16 * f - 16 * e) % 128
+                tail = jnp.where(lane1 // 16 == f, pltpu.roll(v[f], shift, 1) if shift else v[f], tail)
+            out_ref[pl.ds(12 * e + 10 + i, 8, stride=48), :] = jnp.broadcast_to(tail, (8, 128))
+
+
+def carry_kernel(in_ref, out_ref, through_ref, crest_ref):
     sub, lane = sublanes((8, 128)), lanes((8, 128))
-    low_field = jnp.where(sub < 5, sub, 2 * (sub - 5))
-    high_field = jnp.where(sub < 5, sub, jnp.where(sub < 7, 2 * (sub - 5) + 1, 4))
-
-    def pick(row, at):
-        lo = jnp.sum(jnp.where(lane == at + low_field, row, 0.0), axis=1, keepdims=True)
-        hi = jnp.sum(jnp.where(lane == at + high_field, row, 0.0), axis=1, keepdims=True)
-        return jnp.where(lane < 64, lo, hi)
-
-    run, mine = jnp.zeros((8, 128), F32), jnp.zeros((8, 128), F32)
+
+    def gains(row):
+        column = jnp.sum(jnp.where((lane == 96 + sub) & (sub < FIELDS), row, 0.0), axis=1, keepdims=True)
+        spread = jnp.sum(jnp.where(lane // 16 == sub, column, 0.0), axis=0, keepdims=True)
+        return jnp.where(sub < FIELDS, column, spread)
+
+    run = jnp.zeros((8, 128), F32)
     for d in range(WALLS):
-        row = jnp.broadcast_to(in_ref[d, 7:8, :], (8, 128))
-        through, spread = pick(row, 64), pick(row, 72)
+        at = 12 * d
+        up, down = in_ref[at + 10 : at + 11, :], in_ref[at + 11 : at + 12, :]
+        up, down = jnp.broadcast_to(up, (8, 128)), jnp.broadcast_to(down, (8, 128))
+        through = gains(up)
         through_ref[d] = through
-        out_ref[12 * d : 12 * d + 5, :] = run[:5]
-        mine = jnp.where(me == d, run, mine)
-        crest_ref[d] = in_ref[d, 8:, :] + spread * run
-        run = through * run + in_ref[d, :8, :]
-    seam_ref[0] = mine
-    run, mine = jnp.zeros((8, 128), F32), jnp.zeros((8, 128), F32)
+        out_ref[at : at + 5, :] = run[:5]
+        out_ref[at + 10 : at + 11, :] = run[5:6]
+        if d < WALLS - 1:
+            last = in_ref[at + 5 : at + 13, :]
+        else:
+            last = pltpu.roll(in_ref[at + 4 : at + 12, :], 7, 0)
+        crest_ref[d] = jnp.where(sub < FIELDS, last, down) + gains(down) * run
+        run = through * run + jnp.where(sub < FIELDS, in_ref[at : at + 8, :], up)
+    run = jnp.zeros((8, 128), F32)
     for d in reversed(range(WALLS)):
-        out_ref[12 * d + 5 : 12 * d + 10, :] = run[:5]
-        out_ref[12 * d + 10 : 12 * d + 12, :] = jnp.zeros((2, 128), F32)
-        mine = jnp.where(me == d, run, mine)
+        at = 12 * d
+        out_ref[at + 5 : at + 10, :] = run[:5]
+        out_ref[at + 11 : at + 12, :] = run[5:6]
         run = through_ref[d] * run + crest_ref[d]
-    seam_ref[1] = mine
 
 
 def final_kernel(
-    base_ref, ret_ref, seam_ref, low_ref, inv_ref, gain_ref, sp_ref, ext_ref, w_ref, o_ref, fe_ref, fl_ref, in_ref, sc_ref, lhs_ref, res_ref, sem
+    base_ref, ret_ref, low_ref, inv_ref, gain_ref, sp_ref, ext_ref, w_ref, o_ref, fe_ref, fl_ref, in_ref, sc_ref, lhs_ref, res_ref, sem
 ):
     sub, lane = sublanes((8, 128)), lanes((8, 128))
 
-    def unpack(tile):
-        turned = pltpu.roll(tile, 64, 1)
-        a, b = jnp.where(lane < 64, tile, turned), jnp.where(lane < 64, turned, tile)
-        rows = [a[5:6], b[5:6], a[6:7], b[6:7], a[7:8]]
-        out = jnp.broadcast_to(rows[4], (8, 128))
-        for f in range(4):
-            out = jnp.where(sub == f, rows[f], out)
-        return jnp.where(sub < FIELDS, out, 0.0)
-
-    run = unpack(seam_ref[0])
+    def unpack(i):
+        out = jnp.zeros((8, 128), F32)
+        for e in range(4):
+            row = ret_ref[12 * e + 10 + i : 12 * e + 11 + i, :]
+            for f in range(FIELDS):
+                shift = (16 * e - 16 * f) % 128
+                moved = pltpu.roll(row, shift, 1) if shift else row
+                out = jnp.where((sub == f) & (lane // 16 == e), moved, out)
+        return jnp.where(lane < 64, out, pltpu.roll(out, 64, 1))
+
+    run = unpack(0)
     for j in range(ROWS):
         run = ext_ref[j * 8 : j * 8 + 8, :] + run
         fe_ref[j * 8 : j * 8 + 8, :] = run * inv_ref[j * 8 : j * 8 + 8, :]
         run = run * low_ref[j * 8 : j * 8 + 8, :]
-    run = unpack(seam_ref[1])
+    run = unpack(1)
     for j in reversed(range(ROWS)):
         run = fe_ref[j * 8 : j * 8 + 8, :] + low_ref[j * 8 : j * 8 + 8, :] * run
         fe_ref[j * 8 : j * 8 + 8, :] = run * sp_ref[j * 8 : j * 8 + 8, :]
@@ -333,7 +329,7 @@
     from_right = lax.ppermute(left, "stream", [((i + 1) % count, i) for i in range(count)])
     main, base, low, inv, sp = pl.pallas_call(
         sums_kernel,
-        out_shape=[sds((WALLS * 16, 128), F32), sds((FIELDS, ROWS * PLANES, CELLS), F32), rows, rows, rows],
+        out_shape=[sds((WALLS * 12, 128), F32), sds((FIELDS, ROWS * PLANES, CELLS), F32), rows, rows, rows],
         in_specs=[VM] * 5,
         out_specs=[VM] * 5,
         compiler_params=params(),
@@ -342,27 +338,27 @@
     )(cells, fall, lower, pivot, speed)
     send, ext = pl.pallas_call(
         merge_kernel,
-        out_shape=[sds((WALLS, 16, 128), F32), rows],
+        out_shape=[sds((WALLS * 12, 128), F32), rows],
         in_specs=[VM] * 6,
         out_specs=[VM] * 2,
         compiler_params=params(),
         name="merge",
     )(main, rise, fall, unit, from_left, from_right)
-    got = lax.all_to_all(send, "wall", 0, 0, tiled=True)
-    carries, seam = pl.pallas_call(
+    got = lax.all_to_all(send.reshape(WALLS, 3, 4, 128), "wall", 0, 0, tiled=True)
+    carries = pl.pallas_call(
         carry_kernel,
-        out_shape=[sds((WALLS * 12, 128), F32), sds((2, 8, 128), F32)],
+        out_shape=sds((WALLS * 12, 128), F32),
         in_specs=[VM],
-        out_specs=[VM] * 2,
+        out_specs=VM,
         scratch_shapes=[pltpu.VMEM((WALLS, 8, 128), F32)] * 2,
         compiler_params=params(),
         name="carry",
-    )(got)
+    )(got.reshape(WALLS * 12, 128))
     back = lax.all_to_all(carries.reshape(WALLS, 3, 4, 128), "wall", 0, 0, tiled=True)
     out = pl.pallas_call(
         final_kernel,
         out_shape=sds((FIELDS * PLANES, 4, 2, 8, 128), F32),
-        in_specs=[VM] * 9,
+        in_specs=[VM] * 8,
         out_specs=pl.BlockSpec(memory_space=pl.ANY),
         scratch_shapes=[pltpu.VMEM((ROWS * 8 + 8, 128), F32)] * 2
         + [
@@ -374,7 +370,7 @@
         ],
         compiler_params=params(),
         name="final",
-    )(base, back.reshape(WALLS * 12, 128), seam, low, inv, gain, sp, ext, jnp.asarray(stencil))
+    )(base, back.reshape(WALLS * 12, 128), low, inv, gain, sp, ext, jnp.asarray(stencil))
     return out.reshape(FIELDS, PLANES, 4, 2, 8, 128).transpose(0, 1, 2, 4, 3, 5).reshape(FIELDS, PLANES, ROWS, CELLS)
 
 

time: 50.9 us -> 50.3 us (0.988)
  blocking collectives: 29.1 us -> 28.5 us
    all_to_all x1, blocking collectives: 17.3 us -> 16.6 us  [local(): lax.all_to_all(send.reshape(WALLS, 3, 4, 128), 'wall', 0, 0, tiled=True)]
where the time goes in v7:
time: 50.3 us; the launch traced here: 50 us
  blocking collectives  28.5 us (57%)
  starting transfers between devices  14 us (28%)
  Pallas kernels  7.49 us (15%)
    all_to_all x1, blocking collectives, local(): lax.all_to_all(send.reshape(WALLS, 3, 4, 128), 'wall', 0, 0, tiled=True)  16.6 us
    all_to_all x1, blocking collectives, local(): lax.all_to_all(carries.reshape(WALLS, 3, 4, 128), 'wall', 0, 0, tiled=True)  11.8 us
    ppermute x1, starting transfers between devices, local(): lax.ppermute(left, 'stream', [((i + 1) % count, i) for i in range(count)])  9.47 us
    ppermute x1, starting transfers between devices, local(): lax.ppermute(right, 'stream', [(i, (i + 1) % count) for i in range(count)])  4.49 us
    pallas_call x1, Pallas kernels, local(): pl.pallas_call(final_kernel, out_shape=sds((FIELDS * PLANES, 4, 2, 8, 128...  3.34 us
    pallas_call x1, Pallas kernels, local(): pl.pallas_call(edge_kernel, out_shape=[sds((FIELDS, 8, 128), F32)] * 2 +...  2.82 us
  transfers between devices with their start and end apart: 2, of which 0 were waited for; matrix products, arithmetic and copies ran while one was open for 0% of the time, Pallas kernels for 2%

profile of v7, /device:TPU:1, one launch (start us, length us, event | category | flops | bytes accessed | tf_op | source)
XLA Modules:
  0.0 50.0 jit_solution(5985317431248684857)
XLA Ops:
  0.0 0.0 copy-start.2
  0.0 0.0 copy-start.1
  0.0 0.0 copy-start.3
  0.0 2.8 %edge.1 = (f32[5,8,128]{2,1,0:T(8,128)S(1)}, f32[5,8,128]{2,1,0:T(8,128)S(1)}, f32[5,4,2,16,8,128]{5,4,3,2,1,0:T(8,128)S(1)}, f32[264,128]{1,0:T(8,128)S(1)}, f3...) custom-call(f32[5,16,4,2,8,128]{5,4,3,2,1,0:T(8,128)} %bitcast.18, ...), custom_call_target="tpu_custom_call" | custom-call | tf_op jit(solution)/shard_map/edge/pallas_call | solution.py:312
  2.8 0.0 copy-start
  2.9 4.5 %collective-permute-start = (f32[5,8,128]{2,1,0:T(8,128)S(1)}, f32[5,8,128]{2,1,0:T(8,128)S(1)}, u32[]{:S(2)}, u32[]{:S(2)}) collective-permute-start(f32[5,8,128]{2,1,0:T(8,128)S(1)} %get-tuple-element.25), channel_id=1, source_target_pairs={{0,1},{1,2},{2,3},{3,4},{4,5},{5,6},{6,7},{7,8},{8,9},{9,10},{10,1... | collective-permute-start | bytes 61448 | tf_op jit(solution)/shard_map/ppermute | solution.py:328
  7.3 9.5 %collective-permute-start.1 = (f32[5,8,128]{2,1,0:T(8,128)S(1)}, f32[5,8,128]{2,1,0:T(8,128)S(1)}, u32[]{:S(2)}, u32[]{:S(2)}) collective-permute-start(f32[5,8,128]{2,1,0:T(8,128)S(1)} %get-tuple-element.26), channel_id=1, source_target_pairs={{1,0},{2,1},{3,2},{4,3},{5,4},{6,5},{7,6},{8,7},{9,8},{10,9},{11,1... | collective-permute-start | bytes 61448 | tf_op jit(solution)/shard_map/ppermute | solution.py:329
  16.8 0.0 copy-done.2
  16.8 0.0 copy-done.1
  16.8 0.0 copy-done.3
  16.9 0.9 %sums.1 = (f32[384,128]{1,0:T(8,128)S(1)}, f32[5,512,256]{2,1,0:T(8,128)S(1)}, f32[264,128]{1,0:T(8,128)S(1)}, f32[264,128]{1,0:T(8,128)S(1)}, f32[264,128]{1,0:T(8,128)S(1)}) custom-call(f32[5,1024,128]{2,1,0:T(8,128)S(1)} %bitcast.13, f32[264,128]{1,0:T(8,128)S(1)} %get-tuple-element.20.fall_ref, f32[5,32]{1,0:T(8,128)S(1)} %copy-done.1, ...), custom_call_target="tpu_custom_call" | custom-call | flops 4000000 | bytes 2600000 | tf_op jit(solution)/shard_map/sums/pallas_call | solution.py:330
  17.7 0.0 collective-permute-done.left_ref
  17.7 0.0 collective-permute-done.1.right_ref
  17.7 0.3 merge.1
  18.0 16.6 %all_to_all.10 = f32[32,3,4,128]{3,2,1,0:T(4,128)S(1)} all-to-all(f32[32,3,4,128]{3,2,1,0:T(4,128)S(1)} %bitcast.17), channel_id=1, replica_groups=mesh['wall'=32,'stream'=16] {'wall'}, dimensions={0} | all-to-all | bytes 393216 | tf_op jit(solution)/shard_map/all_to_all | solution.py:347
  34.6 0.2 carry.1
  34.9 11.8 %all_to_all.11 = f32[32,3,4,128]{3,2,1,0:T(4,128)S(1)} all-to-all(f32[32,3,4,128]{3,2,1,0:T(4,128)S(1)} %bitcast.16), channel_id=1, replica_groups=mesh['wall'=32,'stream'=16] {'wall'}, dimensions={0} | all-to-all | bytes 393216 | tf_op jit(solution)/shard_map/all_to_all | solution.py:357
  46.7 0.0 copy-done
  46.7 3.3 %final.1 = f32[80,4,2,8,128]{4,3,2,1,0:T(8,128)} custom-call(f32[5,512,256]{2,1,0:T(8,128)S(1)} %get-tuple-element.21.base_ref, f32[384,128]{1,0:T(8,128)S(1)} %bitcast.14, f32[264,128]{1,0:T(8,128)S(1)} %get-tuple-element.28.low_ref, f32[264,128]{1,0:T(8,128)S(1)} %get-tuple-element.29.inv_ref, f32[264,128]{1,0:T(8,128)S(1)} %get-tuple-element.30.gain_ref, ...), custom_call_target="tpu_custom_call" | custom-call | tf_op jit(solution)/shard_map/final/pallas_call | solution.py:358
Async XLA Ops:
  0.0 16.8 %copy-start.2 = (f32[5,32]{1,0:T(8,128)S(1)}, f32[5,32]{1,0:T(8,128)}, u32[]{:S(2)}) copy-start(f32[5,32]{1,0:T(8,128)} %pivot_ref.1) | copy-start | bytes 1924
  0.0 16.8 %copy-start.1 = (f32[5,32]{1,0:T(8,128)S(1)}, f32[5,32]{1,0:T(8,128)}, u32[]{:S(2)}) copy-start(f32[5,32]{1,0:T(8,128)} %lower_ref.1) | copy-start | bytes 1924
  0.0 16.8 %copy-start.3 = (f32[5,32]{1,0:T(8,128)S(1)}, f32[5,32]{1,0:T(8,128)}, u32[]{:S(2)}) copy-start(f32[5,32]{1,0:T(8,128)} %speed_ref.1) | copy-start | bytes 1924
  2.8 43.9 %copy-start = (bf16[1024,256]{1,0:T(8,128)(2,1)S(1)}, bf16[1024,256]{1,0:T(8,128)(2,1)}, u32[]{:S(2)}) copy-start(bf16[1024,256]{1,0:T(8,128)(2,1)} %constant.5.clone.w_ref) | copy-start | bytes 1572868
  2.9 14.9 %collective-permute-start = (f32[5,8,128]{2,1,0:T(8,128)S(1)}, f32[5,8,128]{2,1,0:T(8,128)S(1)}, u32[]{:S(2)}, u32[]{:S(2)}) collective-permute-start(f32[5,8,128]{2,1,0:T(8,128)S(1)} %get-tuple-element.25), channel_id=1, source_target_pairs={{0,1},{1,2},{2,3},{3,4},{4,5},{5,6},{6,7},{7,8},{8,9},{9,10},{10,1... | collective-permute-start | bytes 61448 | tf_op jit(solution)/shard_map/ppermute | solution.py:328
  7.3 10.4 %collective-permute-start.1 = (f32[5,8,128]{2,1,0:T(8,128)S(1)}, f32[5,8,128]{2,1,0:T(8,128)S(1)}, u32[]{:S(2)}, u32[]{:S(2)}) collective-permute-start(f32[5,8,128]{2,1,0:T(8,128)S(1)} %get-tuple-element.26), channel_id=1, source_target_pairs={{1,0},{2,1},{3,2},{4,3},{5,4},{6,5},{7,6},{8,7},{9,8},{10,9},{11,1... | collective-permute-start | bytes 61448 | tf_op jit(solution)/shard_map/ppermute | solution.py:329
